TPU v7x, 128 devices: a whole 4x4x4 slice. The times are simulated.
128 devices in a mesh: slide: 32 (over z, x, core), ctx: 4 (over y).
Axes of the slice: x: 4, y: 4, z: 4, core: 2. Of those that a mesh axis runs over, the one named last changes fastest.
Arguments:
- feature_maps: bfloat16 [4096, 16, 16, 384], P(('slide', 'ctx')), may hold values from -6 to 6
- down_weight: bfloat16 [1536, 768], replicated, may hold values from -0.15625 to 0.15625
- conv_taps: bfloat16 [49, 768], replicated, may hold values from -0.875 to 0.875
- mlp_in: bfloat16 [768, 3072], replicated, may hold values from -0.21875 to 0.21875
- mlp_out: bfloat16 [3072, 768], replicated, may hold values from -0.109375 to 0.109375
- layer_scale: float32 [768], replicated, may hold values from 0.2 to 1
- qkv_weight: bfloat16 [1, 768, 2304], replicated, may hold values from -4.690971 to 4.690971
- out_weight: bfloat16 [1, 768, 768], replicated, may hold values from -0.21875 to 0.21875
- tile_slide: int32 [4096], P(('slide', 'ctx')), may hold values from 0 to 31, as said below
- tile_pos: int32 [4096], P(('slide', 'ctx')), may hold values from 0 to 767, as said below
- slide_len: int32 [32], replicated, may hold values from 1 to 768, as said below
Outputs:
- slide_tokens: bfloat16 [24576, 768], P(('slide', 'ctx'))
Inputs may be any that keep to these rules, and one draw needn't show every extreme that they name: `tile_slide`: the tiles of slide s lie at positions 0 to slide_len[s] - 1 of it, exactly one tile at each. `tile_pos`: among the tiles of one device at most 2 lie in the same block of 192 positions of one slide, and some device has exactly 2 in some block. `slide_len`: the lengths sum to 4096; some slide has exactly 768 tiles.
All inputs are finite; a program needn't handle non-finite values.
Results may differ from a plain program's by a relative error of at most 0.015.
Values may be sent and summed in bfloat16 or wider, within the bound.
A program may use at most 128 MiB of HBM per device.

v0:
```python
import jax
import jax.numpy as jnp
from jax import lax
from jax.sharding import PartitionSpec as P

HEADS = 12
HEAD_DIM = 64
KS = 7
SEQ_DEV = 192


NORM_EPS = 1e-06
FAR_NEGATIVE = -1e30


def layer_norm(values):
    center = values - jnp.mean(values, axis=-1, keepdims=True)
    spread = jnp.mean(center * center, axis=-1, keepdims=True)
    return center * lax.rsqrt(spread + NORM_EPS)


def encode_tiles(tile_maps, down_weight, conv_taps, mlp_in, mlp_out, layer_scale):
    tile_count = tile_maps.shape[0]
    half_side = tile_maps.shape[1] // 2
    chan_count = tile_maps.shape[3]
    model_width = down_weight.shape[1]
    normed = layer_norm(tile_maps.astype(jnp.float32)).astype(jnp.bfloat16)
    patches = normed.reshape(tile_count, half_side, 2, half_side, 2, chan_count).transpose(
        0, 1, 3, 2, 4, 5
    )
    patches = patches.reshape(tile_count * half_side * half_side, 4 * chan_count)
    reduced = jnp.dot(patches, down_weight, preferred_element_type=jnp.float32).astype(jnp.bfloat16)
    widened = reduced.reshape(tile_count, half_side, half_side, model_width).astype(jnp.float32)
    tap_values = conv_taps.astype(jnp.float32)
    pad_reach = KS // 2
    padded = jnp.pad(widened, ((0, 0), (pad_reach, pad_reach), (pad_reach, pad_reach), (0, 0)))
    spatial = jnp.zeros_like(widened)
    for row_off in range(KS):
        for col_off in range(KS):
            spatial = (
                spatial
                + padded[:, row_off : row_off + half_side, col_off : col_off + half_side, :]
                * tap_values[row_off * KS + col_off]
            )
    spatial_normed = (
        layer_norm(spatial)
        .astype(jnp.bfloat16)
        .reshape(tile_count * half_side * half_side, model_width)
    )
    expanded = jax.nn.gelu(
        jnp.dot(spatial_normed, mlp_in, preferred_element_type=jnp.float32), approximate=False
    ).astype(jnp.bfloat16)
    branch = jnp.dot(expanded, mlp_out, preferred_element_type=jnp.float32)
    blocked = widened + (layer_scale * branch).reshape(
        tile_count, half_side, half_side, model_width
    )
    pooled = jnp.mean(blocked, axis=(1, 2))
    return layer_norm(pooled).astype(jnp.bfloat16)


def shards(
    feature_maps,
    down_weight,
    conv_taps,
    mlp_in,
    mlp_out,
    layer_scale,
    qkv_weight,
    out_weight,
    tile_slide,
    tile_pos,
    slide_len,
):
    slide_count = lax.axis_size("slide")
    ctx_count = lax.axis_size("ctx")
    device_count = slide_count * ctx_count
    capacity = (SEQ_DEV + device_count - 1) // device_count
    buffer_rows = device_count * capacity
    model_width = qkv_weight.shape[1]
    tiles_here = feature_maps.shape[0]
    embeds = encode_tiles(feature_maps, down_weight, conv_taps, mlp_in, mlp_out, layer_scale)
    owner_index = tile_slide * ctx_count + tile_pos // SEQ_DEV
    tile_order = jnp.arange(tiles_here, dtype=jnp.int32)
    earlier = (owner_index[None, :] == owner_index[:, None]) & (
        tile_order[None, :] < tile_order[:, None]
    )
    tile_rank = jnp.sum(earlier.astype(jnp.int32), axis=1)
    target_row = owner_index * capacity + tile_rank
    placing = jnp.arange(buffer_rows, dtype=jnp.int32)[:, None] == target_row[None, :]
    outgoing = jnp.dot(
        placing.astype(jnp.bfloat16), embeds, preferred_element_type=jnp.float32
    ).astype(jnp.bfloat16)
    local_slot = tile_pos % SEQ_DEV
    slot_sent = jnp.sum(jnp.where(placing, local_slot[None, :] + 1, 0), axis=1) - 1
    slot_sent = jnp.where(slot_sent < 0, SEQ_DEV, slot_sent)
    arrived, arrived_slot = (
        lax.all_to_all(outgoing, ("slide", "ctx"), split_axis=0, concat_axis=0, tiled=True),
        lax.all_to_all(slot_sent, ("slide", "ctx"), split_axis=0, concat_axis=0, tiled=True),
    )
    position = jnp.arange(SEQ_DEV, dtype=jnp.int32)
    picking = (position[:, None] == arrived_slot[None, :]).astype(jnp.bfloat16)
    slot_rows = jnp.dot(picking, arrived, preferred_element_type=jnp.float32).astype(jnp.bfloat16)
    stream = slot_rows.astype(jnp.float32)
    length = slide_len[lax.axis_index("slide")]
    query_pos = lax.axis_index("ctx") * SEQ_DEV + position
    score_scale = HEAD_DIM ** (-0.5)
    lnorm = layer_norm(stream).astype(jnp.bfloat16)
    query_weight = qkv_weight[0, :, :model_width]
    key_weight = qkv_weight[0, :, model_width:]
    queries = jnp.dot(lnorm, query_weight, preferred_element_type=jnp.float32).astype(jnp.bfloat16)
    queries = queries.reshape(SEQ_DEV, HEADS, HEAD_DIM)
    local_kv = jnp.dot(lnorm, key_weight, preferred_element_type=jnp.float32).astype(jnp.bfloat16)
    key_rows = lax.all_gather(local_kv, "ctx", axis=0, tiled=True)
    running_max = jnp.full((HEADS, SEQ_DEV), FAR_NEGATIVE, jnp.float32)
    row_count = key_rows.shape[0]
    keys_part = key_rows[:, :model_width].reshape(row_count, HEADS, HEAD_DIM)
    values_part = key_rows[:, model_width:].reshape(row_count, HEADS, HEAD_DIM)
    scores = (
        jnp.einsum("qhe,khe->hqk", queries, keys_part, preferred_element_type=jnp.float32)
        * score_scale
    )
    included = jnp.arange(row_count, dtype=jnp.int32) < length
    scores = jnp.where(included[None, None, :], scores, FAR_NEGATIVE)
    new_max = jnp.maximum(running_max, jnp.max(scores, axis=-1))
    weights = jnp.where(included[None, None, :], jnp.exp(scores - new_max[:, :, None]), 0.0)
    denom_sum = jnp.sum(weights, axis=-1)
    accum = jnp.einsum(
        "hqk,khe->hqe",
        weights.astype(jnp.bfloat16),
        values_part,
        preferred_element_type=jnp.float32,
    )
    folded = (new_max, denom_sum, accum)
    running_max, denom_sum, accum = folded
    attended = (accum / denom_sum[:, :, None]).transpose(1, 0, 2).reshape(SEQ_DEV, model_width)
    attended = attended.astype(jnp.bfloat16)
    stream = stream + jnp.dot(attended, out_weight[0], preferred_element_type=jnp.float32)
    valid_rows = query_pos < length
    return jnp.where(valid_rows[:, None], stream, 0.0).astype(jnp.bfloat16)


def solution(mesh):
    return jax.shard_map(
        shards,
        mesh=mesh,
        in_specs=(
            P(("slide", "ctx"), None, None, None),
            P(),
            P(),
            P(),
            P(),
            P(),
            P(),
            P(),
            P(("slide", "ctx")),
            P(("slide", "ctx")),
            P(),
        ),
        out_specs=P(("slide", "ctx"), None),
        check_vma=False,
    )
```

profile of v0, /device:TPU:1, one launch (start us, length us, event | category | flops | bytes accessed | tf_op | source)
XLA Modules:
  0.0 364.7 jit_solution(13976290073714128194)
XLA Ops:
  6.5 0.8 fusion.146
  8.9 12.0 %all-to-all-start = ((s32[128,2,1]{1,2,0:T(1,128)}), s32[128,2,1]{1,2,0:T(1,128)}, u32[]{:S(2)}, u32[]{:S(2)}) async-start(s32[128,2,1]{1,2,0:T(1,128)} %bitcast.1), calls=%async_computation | async-start | bytes 131072 | tf_op jit(solution)/shard_map/all_to_all | solution.py:98
  20.9 1.1 convert_element_type.70
  22.4 4.3 %convert_reduce_fusion = f32[32,16,16]{2,1,0:T(8,128)S(1)} fusion(bf16[32,16,16,384]{3,2,1,0:T(8,128)(2,1)} %param.11), kind=kLoop, calls=%fused_computation.68 | loop fusion | flops 6283264 | bytes 6324224 | tf_op jit(solution)/shard_map/reduce_sum | solution.py:17
  26.8 3.1 fusion.12
  30.0 4.3 %fusion.13 = bf16[32,16,16,384]{3,2,1,0:T(8,128)(2,1)} fusion(bf16[32,16,16,384]{3,2,1,0:T(8,128)(2,1)S(1)} %copy-done.2, f32[32,16,16]{2,1,0:T(8,128)S(1)} %add_rsqrt_fusion, f32[32,16,16]{2,1,0:T(8,128)S(1)} %broadcast_multiply_fusion), kind=kLoop, calls=%fused_computation.72 | loop fusion | flops 12582912 | bytes 12648448 | tf_op jit(solution)/shard_map/convert_element_type | solution.py:27
  34.2 13.3 %reshape.166 = bf16[32,8,2,8,2,384]{5,4,3,2,1,0:T(2,128)(2,1)} reshape(bf16[32,16,16,384]{3,2,1,0:T(8,128)(2,1)} %fusion.13) | data formatting | bytes 12582912 | tf_op jit(solution)/shard_map/reshape | solution.py:28
  47.5 6.9 %copy.30 = bf16[32,8,2,8,2,384]{5,4,2,3,1,0:T(2,128)(2,1)} copy(bf16[32,8,2,8,2,384]{5,4,3,2,1,0:T(2,128)(2,1)} %reshape.166) | data formatting | bytes 12582912 | tf_op jit(solution)/shard_map/reshape | solution.py:28
  54.4 14.4 %reshape.167 = bf16[2048,1536]{1,0:T(8,128)(2,1)} reshape(bf16[32,8,8,2,2,384]{5,4,3,2,1,0:T(2,128)(2,1)} %bitcast.55) | data formatting | bytes 12582912 | tf_op jit(solution)/shard_map/reshape | solution.py:31
  68.8 8.2 %convolution_convert_fusion = bf16[2048,768]{1,0:T(8,128)(2,1)S(1)} fusion(bf16[2048,1536]{1,0:T(8,128)(2,1)} %reshape.167, bf16[1536,768]{1,0:T(8,128)(2,1)S(1)} %copy-done), kind=kOutput, calls=%fused_computation.183 | convolution fusion | flops 4833411072 | bytes 11796480 | tf_op jit(solution)/shard_map/dot_general | solution.py:32
  77.0 1.7 copy-done.5
  78.7 3.4 bitcast_convert_fusion
  82.1 120.8 %fusion.184 = (f32[32,8,8]{2,1,0:T(8,128)S(1)}, f32[32,8,8,768]{3,2,1,0:T(8,128)}) fusion(f32[768]{0:T(1024)S(1)} %get-tuple-element.6, f32[768]{0:T(1024)S(1)} %get-tuple-element.7, f32[768]{0:T(1024)S(1)} %get-tuple-element.8, f32[768]{0:T(1024)S(1)} %get-tuple-element.9, f32[768]{0:T(1024)S(1)} %get-tuple-element.10, f32[768]{0:T(1024)S(1)} %get-tuple-element.11, ...), kind=kLoop, calls=%fused_computation.317 | loop fusion | flops 154138624 | bytes 12741632 | tf_op jit(solution)/shard_map/reduce_sum | solution.py:17
  203.0 3.7 %multiply_reduce_fusion = f32[32,8,8]{2,1,0:T(8,128)S(1)} fusion(f32[32,8,8,768]{3,2,1,0:T(8,128)} %get-tuple-element.55, f32[32,8,8]{2,1,0:T(8,128)S(1)} %broadcast_multiply_fusion.1), kind=kLoop, calls=%fused_computation.176 | loop fusion | flops 4716544 | bytes 6307840 | tf_op jit(solution)/shard_map/reduce_sum | solution.py:18
  206.8 0.8 copy-done.3
  207.6 0.8 multiply_convert_fusion
  209.2 62.4 %fusion.207 = bf16[2048,3072]{1,0:T(8,128)(2,1)S(1)} fusion(bf16[2048,768]{1,0:T(8,128)(2,1)S(1)} %bitcast.57, bf16[768,3072]{1,0:T(8,128)(2,1)S(1)} %bitcast.63), kind=kOutput, calls=%fused_computation.51.clone.clone.clone.clone.clone.clone.1 | convolution fusion | flops 10072621056 | bytes 20447232 | tf_op jit(solution)/shard_map/dot_general | solution.py:51
  271.6 10.2 %add_reduce_fusion = f32[32,768]{1,0:T(8,128)S(1)} fusion(bf16[2048,768]{1,0:T(8,128)(2,1)S(1)} %copy-done.6, bf16[3072,768]{1,0:T(8,128)(2,1)S(1)} %copy-done.10, f32[768]{0:T(1024)S(1)} %copy-done.11, bf16[2048,3072]{1,0:T(8,128)(2,1)S(1)} %fusion.207), kind=kOutput, calls=%fused_computation.174 | convolution fusion | flops 9669943296 | bytes 20548608 | tf_op jit(solution)/shard_map/dot_general | solution.py:53
  282.6 0.9 all_to_all.13
  283.5 9.8 %all-to-all-start.1 = ((bf16[128,2,768]{2,1,0:T(2,128)(2,1)}), bf16[128,2,768]{2,1,0:T(2,128)(2,1)S(1)}, u32[]{:S(2)}, u32[]{:S(2)}) async-start(bf16[128,2,768]{2,1,0:T(2,128)(2,1)} %all_to_all.13), calls=%async_computation.1 | async-start | bytes 786432 | tf_op jit(solution)/shard_map/all_to_all | solution.py:97
  293.8 1.6 reduce.101
  295.6 10.0 %all-to-all-done.1 = bf16[128,2,768]{2,1,0:T(2,128)(2,1)S(1)} async-done(((bf16[128,2,768]{2,1,0:T(2,128)(2,1)}), bf16[128,2,768]{2,1,0:T(2,128)(2,1)S(1)}, u32[]{:S(2)}, u32[]{:S(2)}) %all-to-all-start.1) | async-done | bytes 393248 | tf_op jit(solution)/shard_map/all_to_all | solution.py:97
  306.4 3.2 convolution_convert_fusion.1
  311.5 1.7 convolution_convert_fusion.3
  313.4 25.1 %all-gather.2.cloned.1.call-done = bf16[768,1536]{1,0:T(8,128)(2,1)} async-done(((bf16[192,1536]{1,0:T(8,128)(2,1)}), bf16[768,1536]{1,0:T(8,128)(2,1)}) %all-gather.2.cloned.1.call-update) | async-done | bytes 2359312 | tf_op jit(solution)/shard_map/all_gather | solution.py:113
  338.5 2.8 fusion.186
  341.3 1.6 copy.27
  342.8 4.1 %fusion.114 = (f32[12,192]{1,0:T(8,128)S(1)}, f32[12,192,768]{2,1,0:T(8,128)}) fusion(pred[768]{0:T(1024)(128)(4,1)S(1)} %iota_compare_fusion.5, bf16[192,12,64]{0,2,1:T(8,128)(2,1)S(1)} %bitcast.58, bf16[768,12,64]{0,2,1:T(8,128)(2,1)S(1)} %bitcast.56), kind=kOutput, calls=%fused_computation.177 | convolution fusion | flops 231798528 | bytes 8562432 | tf_op jit(solution)/shard_map/qhe,khe->hqk/dot_general | solution.py:119
  346.9 1.4 copy.28
  348.4 4.6 %fusion.115 = f32[12,192]{1,0:T(8,128)S(1)} fusion(f32[12,192,768]{2,1,0:T(8,128)} %get-tuple-element.63, f32[12,192]{1,0:T(8,128)S(1)} %broadcast_maximum_fusion, pred[768]{0:T(1024)(128)(4,1)S(1)} %iota_compare_fusion.5), kind=kLoop, calls=%fused_computation.178 | loop fusion | flops 8845056 | bytes 7097088 | tf_op jit(solution)/shard_map/reduce_sum | solution.py:126
  353.4 3.3 fusion.137
  356.7 1.1 fusion.130
  (62 shorter events, 7.6 us)
Async XLA Ops:
  6.5 62.3 %copy-start = (bf16[1536,768]{1,0:T(8,128)(2,1)S(1)}, bf16[1536,768]{1,0:T(8,128)(2,1)}, u32[]{:S(2)}) copy-start(bf16[1536,768]{1,0:T(8,128)(2,1)} %param.12) | copy-start | bytes 7077892
  7.6 0.6 copy-start.8
  8.9 274.5 %all-to-all-start = ((s32[128,2,1]{1,2,0:T(1,128)}), s32[128,2,1]{1,2,0:T(1,128)}, u32[]{:S(2)}, u32[]{:S(2)}) async-start(s32[128,2,1]{1,2,0:T(1,128)} %bitcast.1), calls=%async_computation | async-start | bytes 131072 | tf_op jit(solution)/shard_map/all_to_all | solution.py:98
  20.9 5.8 %copy-start.2 = (bf16[32,16,16,384]{3,2,1,0:T(8,128)(2,1)S(1)}, bf16[32,16,16,384]{3,2,1,0:T(8,128)(2,1)}, u32[]{:S(2)}) copy-start(bf16[32,16,16,384]{3,2,1,0:T(8,128)(2,1)} %param.11) | copy-start | bytes 18874372
  77.0 1.7 copy-start.5
  203.0 4.6 %copy-start.3 = (f32[32,8,8,768]{3,2,1,0:T(8,128)S(1)}, f32[32,8,8,768]{3,2,1,0:T(8,128)}, u32[]{:S(2)}) copy-start(f32[32,8,8,768]{3,2,1,0:T(8,128)} %get-tuple-element.55) | copy-start | bytes 18874372
  206.7 2.4 slice-start
  207.6 1.6 slice-start.1
  209.2 62.4 %copy-start.6 = (bf16[2048,768]{1,0:T(8,128)(2,1)S(1)}, bf16[2048,768]{1,0:T(8,128)(2,1)}, u32[]{:S(2)}) copy-start(bf16[2048,768]{1,0:T(8,128)(2,1)} %copy-done.5) | copy-start | bytes 9437188
  209.2 62.4 %copy-start.10 = (bf16[3072,768]{1,0:T(8,128)(2,1)S(1)}, bf16[3072,768]{1,0:T(8,128)(2,1)}, u32[]{:S(2)}) copy-start(bf16[3072,768]{1,0:T(8,128)(2,1)} %param.15) | copy-start | bytes 14155780
  209.2 62.4 %copy-start.11 = (f32[768]{0:T(1024)S(1)}, f32[768]{0:T(1024)}, u32[]{:S(2)}) copy-start(f32[768]{0:T(1024)} %param.16) | copy-start | bytes 9220
  271.6 10.6 %copy-start.9 = (s32[32]{0:T(128)S(1)}, s32[32]{0:T(128)}, u32[]{:S(2)}) copy-start(s32[32]{0:T(128)} %copy-done.8) | copy-start | bytes 388
  281.9 27.7 %copy-start.12 = (s32[32]{0:T(128)S(1)}, s32[32]{0:T(128)}, u32[]{:S(2)}) copy-start(s32[32]{0:T(128)} %param.21) | copy-start | bytes 388
  283.5 22.1 %all-to-all-start.1 = ((bf16[128,2,768]{2,1,0:T(2,128)(2,1)}), bf16[128,2,768]{2,1,0:T(2,128)(2,1)S(1)}, u32[]{:S(2)}, u32[]{:S(2)}) async-start(bf16[128,2,768]{2,1,0:T(2,128)(2,1)} %all_to_all.13), calls=%async_computation.1 | async-start | bytes 786432 | tf_op jit(solution)/shard_map/all_to_all | solution.py:97
  293.2 45.2 %all-gather.2.cloned.1.call-start = ((), (), s32[]{:S(2)}) async-start(), calls=%async_computation.2 | async-start | bytes 2949120 | tf_op jit(solution)/shard_map/all_gather | solution.py:113
  348.4 5.1 %copy-start.4 = (f32[12,192,768]{2,1,0:T(8,128)S(1)}, f32[12,192,768]{2,1,0:T(8,128)}, u32[]{:S(2)}) copy-start(f32[12,192,768]{2,1,0:T(8,128)} %get-tuple-element.63) | copy-start | bytes 21233668
  352.9 4.9 %copy-start.1 = (bf16[1536,768]{1,0:T(8,128)(2,1)S(1)}, bf16[1536,768]{1,0:T(8,128)(2,1)}, u32[]{:S(2)}) copy-start(bf16[1536,768]{1,0:T(8,128)(2,1)} %param.12) | copy-start | bytes 7077892
  353.4 3.3 copy-start.7
Sparse Core Ops, SparseCore 0:
  309.7 28.7 all-gather.1
where the time goes:
time: 366 us; the launch traced here: 365 us
  other arithmetic  151 us (41%)
  matrix products  94.9 us (26%)
  local copies, waits for them, and re-layouts  47.7 us (13%)
  waiting for transfers between devices  35.1 us (10%)
  starting transfers between devices  21.8 us (6%)
  between operations  13.7 us (4%)
    reduce_sum x3, other arithmetic, layer_norm(): center = values - jnp.mean(values, axis=-1, keepdims=True)  125 us
    dot_general x1, matrix products, encode_tiles(): jnp.dot(spatial_normed, mlp_in, preferred_element_type=jnp.float32)  62.4 us
    all_gather x1, waiting for transfers between devices, shards(): key_rows = lax.all_gather(local_kv, 'ctx', axis=0, tiled=True)  25.1 us
    reshape x2, local copies, waits for them, and re-layouts, encode_tiles(): normed.reshape(tile_count, half_side, 2, half_side, 2, chan_count)  20.1 us
    reshape x1, local copies, waits for them, and re-layouts, encode_tiles(): patches.reshape(tile_count * half_side * half_side, 4 * chan_count)  14.4 us
    all_to_all x1, starting transfers between devices, shards(): lax.all_to_all(slot_sent, ('slide', 'ctx'), split_axis=0, concat_axis=0,...  12 us
    dot_general x1, matrix products, encode_tiles(): branch = jnp.dot(expanded, mlp_out, preferred_element_type=jnp.float32)  10.2 us
    all_to_all x1, waiting for transfers between devices, shards(): lax.all_to_all(outgoing, ('slide', 'ctx'), split_axis=0, concat_axis=0, t...  10 us
  transfers between devices with their start and end apart: 3, of which 2 were waited for; matrix products, arithmetic and copies ran while one was open for 72% of the time, Pallas kernels for 0%

commit v1 on v0

v1 whole, which is shorter than its diff:
```python
import jax
import jax.numpy as jnp
from jax import lax
from jax.experimental import pallas as pl
from jax.experimental.pallas import tpu as pltpu

NORM_EPS = 1e-06
GROUP = 8
HALF = 8
KS = 7
C_IN = 384
D = 768
LB = D // 128
MLP = 3072
HC = 512
PITCH = 257
UA = 4
UD = 4
INV_SQRT2 = 0.7071067811865476

def double_gelu(v):
    return v + v * lax.erf(v * INV_SQRT2)

def encode_kernel(x_ref, down_ref, taps_ref, w1_ref, w2_ref, ls_ref, out_ref,
                  s_ref, l_ref, r_ref, sp_ref, sn_ref, tap_ref, ph_ref, pr_ref):
    g = pl.program_id(0)

    @pl.when(g == 0)
    def _():
        t = taps_ref[...].astype(jnp.float32)
        for k in range(KS * KS):
            for l in range(LB):
                tap_ref[l, k] = jnp.broadcast_to(t[k:k + 1, l * 128:(l + 1) * 128], (8, 128))

    def norm_rows(n, _):
        t = n // 4
        y = (n % 4) * 4
        x = x_ref[t, pl.ds(y, 4)].reshape(64, C_IN).astype(jnp.float32)
        c = x - jnp.mean(x, axis=-1, keepdims=True)
        v = jnp.mean(c * c, axis=-1, keepdims=True)
        o = c * lax.rsqrt(v + NORM_EPS)
        base = t * PITCH + y * 16
        for l in range(3):
            s_ref[l, pl.ds(base, 64), :] = o[:, l * 128:(l + 1) * 128]
        return 0
    lax.fori_loop(0, GROUP * 4, norm_rows, 0, unroll=UA)

    def patch_rows(n, _):
        i = n // 4
        jp = (n % 4) * 2
        row = pl.multiple_of((i * HALF + jp) * GROUP, 16)
        for dy in range(2):
            for dx in range(2):
                for l in range(3):
                    pos = (2 * i + dy) * 16 + 2 * jp + dx
                    a = s_ref[l, pl.ds(pos, GROUP, stride=PITCH), :]
                    b = s_ref[l, pl.ds(pos + 2, GROUP, stride=PITCH), :]
                    col = (dy * 2 + dx) * C_IN + l * 128
                    l_ref[pl.ds(row, 16), col:col + 128] = jnp.concatenate([a, b], axis=0).astype(jnp.bfloat16)
        return 0
    lax.fori_loop(0, HALF * HALF // 2, patch_rows, 0, unroll=2)

    for n in range(3):
        red = jnp.dot(l_ref[...], down_ref[:, n * 256:(n + 1) * 256], preferred_element_type=jnp.float32)
        red = red.astype(jnp.bfloat16).astype(jnp.float32)
        for h in range(2):
            r_ref[n * 2 + h] = red[:, h * 128:(h + 1) * 128].reshape(64, GROUP, 128)

    def conv_lane(l, _):
        psum = jnp.zeros((GROUP, 128), jnp.float32)
        for i in range(HALF):
            acc = [None] * HALF
            for a in range(KS):
                ii = i + a - 3
                if not 0 <= ii < HALF:
                    continue
                xs = [r_ref[l, ii * HALF + j] for j in range(HALF)]
                for b in range(KS):
                    w = tap_ref[l, a * KS + b]
                    for j in range(HALF):
                        jj = j + b - 3
                        if 0 <= jj < HALF:
                            term = xs[jj] * w
                            acc[j] = term if acc[j] is None else acc[j] + term
                if ii == i:
                    for j in range(HALF):
                        psum = psum + xs[j]
            for j in range(HALF):
                sp_ref[l, i * HALF + j] = acc[j]
        pr_ref[l, pl.ds(pl.multiple_of(g * GROUP, GROUP), GROUP), :] = psum
        return 0
    lax.fori_loop(0, LB, conv_lane, 0)

    def norm_spatial(n, _):
        rows = [sp_ref[l, pl.ds(n * 8, 8)].reshape(64, 128) for l in range(LB)]
        tot = rows[0]
        for r in rows[1:]:
            tot = tot + r
        mean = jnp.sum(tot, axis=-1, keepdims=True) * (1.0 / D)
        cs = [r - mean for r in rows]
        sq = cs[0] * cs[0]
        for c in cs[1:]:
            sq = sq + c * c
        var = jnp.sum(sq, axis=-1, keepdims=True) * (1.0 / D)
        inv = lax.rsqrt(var + NORM_EPS)
        for l in range(LB):
            sn_ref[pl.ds(pl.multiple_of(n * 64, 64), 64), l * 128:(l + 1) * 128] = (cs[l] * inv).astype(jnp.bfloat16)
        return 0
    lax.fori_loop(0, 8, norm_spatial, 0, unroll=UD)

    for c in range(MLP // HC):
        h = jnp.dot(sn_ref[...], w1_ref[:, c * HC:(c + 1) * HC], preferred_element_type=jnp.float32)
        h = double_gelu(h)
        ph_ref[pl.ds(pl.multiple_of(g * GROUP, GROUP), GROUP), c * HC:(c + 1) * HC] = jnp.sum(
            h.reshape(64, GROUP, HC), axis=0)

    @pl.when(g == pl.num_programs(0) - 1)
    def _():
        p = ph_ref[...]
        hi = p.astype(jnp.bfloat16)
        lo = (p - hi.astype(jnp.float32)).astype(jnp.bfloat16)
        br = jnp.dot(jnp.concatenate([hi, lo], axis=0), w2_ref[...], preferred_element_type=jnp.float32)
        nt = p.shape[0]
        br = br[:nt] + br[nt:]
        pr = jnp.concatenate([pr_ref[l] for l in range(LB)], axis=-1)
        pooled = (pr + ls_ref[...] * (0.5 * br)) * (1.0 / 64)
        c = pooled - jnp.mean(pooled, axis=-1, keepdims=True)
        v = jnp.mean(c * c, axis=-1, keepdims=True)
        out_ref[...] = (c * lax.rsqrt(v + NORM_EPS)).astype(jnp.bfloat16)

def encode_tiles(x, down, taps, w1, w2, ls):
    nt = x.shape[0]
    one = pl.Buffered(1)
    full = lambda s: pl.BlockSpec(s, lambda g: (0,) * len(s), pipeline_mode=one)
    return pl.pallas_call(
        encode_kernel,
        out_shape=jax.ShapeDtypeStruct((nt, D), jnp.bfloat16),
        grid=(nt // GROUP,),
        in_specs=[
            pl.BlockSpec((GROUP, 16, 16, C_IN), lambda g: (g, 0, 0, 0)),
            full((4 * C_IN, D)), full((KS * KS, D)), full((D, MLP)), full((MLP, D)), full((1, D)),
        ],
        out_specs=pl.BlockSpec((nt, D), lambda g: (0, 0)),
        scratch_shapes=[
            pltpu.VMEM((3, GROUP * PITCH, 128), jnp.float32),
            pltpu.VMEM((64 * GROUP, 4 * C_IN), jnp.bfloat16),
            pltpu.VMEM((LB, 64, GROUP, 128), jnp.float32),
            pltpu.VMEM((LB, 64, GROUP, 128), jnp.float32),
            pltpu.VMEM((64 * GROUP, D), jnp.bfloat16),
            pltpu.VMEM((LB, KS * KS, 8, 128), jnp.float32),
            pltpu.VMEM((nt, MLP), jnp.float32),
            pltpu.VMEM((LB, nt, 128), jnp.float32),
        ],
        compiler_params=pltpu.CompilerParams(vmem_limit_bytes=56 << 20),
        name="encode",
    )(x, down, taps, w1, w2, ls.reshape(1, D))


from jax.sharding import PartitionSpec as P

HEADS = 12
HEAD_DIM = 64
SEQ_DEV = 192
FAR_NEGATIVE = -1e30


def layer_norm(values):
    center = values - jnp.mean(values, axis=-1, keepdims=True)
    spread = jnp.mean(center * center, axis=-1, keepdims=True)
    return center * lax.rsqrt(spread + NORM_EPS)


def shards(feature_maps, down_weight, conv_taps, mlp_in, mlp_out, layer_scale, qkv_weight, out_weight,
           tile_slide, tile_pos, slide_len):
    ctx_count = lax.axis_size("ctx")
    device_count = lax.axis_size("slide") * ctx_count
    capacity = (SEQ_DEV + device_count - 1) // device_count
    tiles_here = feature_maps.shape[0]
    embeds = encode_tiles(feature_maps, down_weight, conv_taps, mlp_in, mlp_out, layer_scale)
    owner_index = tile_slide * ctx_count + tile_pos // SEQ_DEV
    tile_order = jnp.arange(tiles_here, dtype=jnp.int32)
    earlier = (owner_index[None, :] == owner_index[:, None]) & (tile_order[None, :] < tile_order[:, None])
    tile_rank = jnp.sum(earlier.astype(jnp.int32), axis=1)
    target_row = owner_index * capacity + tile_rank
    placing = jnp.arange(device_count * capacity, dtype=jnp.int32)[:, None] == target_row[None, :]
    slot_code = (tile_pos % SEQ_DEV + 1).astype(jnp.bfloat16)
    coded = jnp.concatenate([embeds, jnp.broadcast_to(slot_code[:, None], (tiles_here, 128))], axis=1)
    outgoing = jnp.dot(placing.astype(jnp.bfloat16), coded, preferred_element_type=jnp.float32).astype(jnp.bfloat16)
    arrived = lax.all_to_all(outgoing, ("slide", "ctx"), split_axis=0, concat_axis=0, tiled=True)
    arrived_slot = arrived[:, D].astype(jnp.int32) - 1
    position = jnp.arange(SEQ_DEV, dtype=jnp.int32)
    picking = (position[:, None] == arrived_slot[None, :]).astype(jnp.bfloat16)
    slot_rows = jnp.dot(picking, arrived[:, :D], preferred_element_type=jnp.float32).astype(jnp.bfloat16)
    all_rows = lax.all_gather(slot_rows, "ctx", axis=0, tiled=True)
    length = slide_len[lax.axis_index("slide")]
    query_pos = lax.axis_index("ctx") * SEQ_DEV + position
    stream = slot_rows.astype(jnp.float32)
    lnorm = layer_norm(stream).astype(jnp.bfloat16)
    lnorm_all = layer_norm(all_rows.astype(jnp.float32)).astype(jnp.bfloat16)
    queries = jnp.dot(lnorm, qkv_weight[0, :, :D], preferred_element_type=jnp.float32).astype(jnp.bfloat16)
    queries = queries.reshape(SEQ_DEV, HEADS, HEAD_DIM)
    key_rows = jnp.dot(lnorm_all, qkv_weight[0, :, D:], preferred_element_type=jnp.float32).astype(jnp.bfloat16)
    row_count = key_rows.shape[0]
    keys_part = key_rows[:, :D].reshape(row_count, HEADS, HEAD_DIM)
    values_part = key_rows[:, D:].reshape(row_count, HEADS, HEAD_DIM)
    scores = jnp.einsum("qhe,khe->hqk", queries, keys_part, preferred_element_type=jnp.float32) * HEAD_DIM ** (-0.5)
    included = jnp.arange(row_count, dtype=jnp.int32) < length
    scores = jnp.where(included[None, None, :], scores, FAR_NEGATIVE)
    peak = jnp.max(scores, axis=-1)
    weights = jnp.where(included[None, None, :], jnp.exp(scores - peak[:, :, None]), 0.0)
    denom_sum = jnp.sum(weights, axis=-1)
    accum = jnp.einsum("hqk,khe->hqe", weights.astype(jnp.bfloat16), values_part, preferred_element_type=jnp.float32)
    attended = (accum / denom_sum[:, :, None]).transpose(1, 0, 2).reshape(SEQ_DEV, D).astype(jnp.bfloat16)
    stream = stream + jnp.dot(attended, out_weight[0], preferred_element_type=jnp.float32)
    return jnp.where((query_pos < length)[:, None], stream, 0.0).astype(jnp.bfloat16)


def solution(mesh):
    whole = P(("slide", "ctx"))
    return jax.shard_map(
        shards,
        mesh=mesh,
        in_specs=(whole, P(), P(), P(), P(), P(), P(), P(), whole, whole, P()),
        out_specs=whole,
        check_vma=False,
    )
```

time: 366 us -> 135 us (0.37)
  other arithmetic: 151 us -> 6.88 us
  matrix products: 94.9 us -> 18.2 us
  Pallas kernels: 0 us -> 51.9 us
  local copies, waits for them, and re-layouts: 47.7 us -> 6.35 us
  blocking collectives: 0 us -> 24.3 us
  starting transfers between devices: 21.8 us -> 0.01 us
  waiting for transfers between devices: 35.1 us -> 13.4 us
    reduce_sum x3 -> x1, other arithmetic: 125 us -> 1.59 us  [layer_norm(): center = values - jnp.mean(values, axis=-1, keepdims=True)]
    dot_general x8 -> x4, matrix products: 90.5 us -> 7.59 us  [the longest x1 3.76 us: shards(): jnp.dot(lnorm_all, qkv_weight[0, :, D:], preferred_element_type=jnp.float32)]
    pallas_call x0 -> x1, Pallas kernels: none -> 51.9 us  [encode_tiles(): pl.pallas_call(encode_kernel, out_shape=jax.ShapeDtypeStruct((nt, D), jnp...]
    reshape x3 -> x1, local copies, waits for them, and re-layouts: 34.6 us -> 1.29 us  [encode_tiles(): ls.reshape(1, D)]
    all_to_all x0 -> x1, blocking collectives: none -> 24.3 us  [shards(): lax.all_to_all(outgoing, ('slide', 'ctx'), split_axis=0, concat_axis=0, t...]
    all_to_all x2 -> x0, starting transfers between devices: 21.7 us -> none  [the longest x1 12 us: shards(): lax.all_to_all(slot_sent, ('slide', 'ctx'), split_axis=0, concat_axis=0,...]
    all_gather x1, waiting for transfers between devices: 25.1 us -> 13.4 us  [shards(): all_rows = lax.all_gather(slot_rows, 'ctx', axis=0, tiled=True)]
    all_to_all x2 -> x0, waiting for transfers between devices: 10 us -> none  [the longest x1 10 us: shards(): lax.all_to_all(outgoing, ('slide', 'ctx'), split_axis=0, concat_axis=0, t...]
  transfers between devices with their start and end apart: 3 -> 1, of which waited for: 2 -> 1; matrix products, arithmetic and copies ran while one was open for 72% -> 4% of each run, Pallas kernels for 0% -> 0%
where the time goes in v1:
time: 135 us
  Pallas kernels  51.9 us (38%)
  blocking collectives  24.3 us (18%)
  matrix products  18.2 us (13%)
  between operations  13.5 us (10%)
  waiting for transfers between devices  13.4 us (10%)
  other arithmetic  6.88 us (5%)
  local copies, waits for them, and re-layouts  6.35 us (5%)
    pallas_call x1, Pallas kernels, encode_tiles(): pl.pallas_call(encode_kernel, out_shape=jax.ShapeDtypeStruct((nt, D), jnp...  51.9 us
    all_to_all x1, blocking collectives, shards(): lax.all_to_all(outgoing, ('slide', 'ctx'), split_axis=0, concat_axis=0, t...  24.3 us
    all_gather x1, waiting for transfers between devices, shards(): all_rows = lax.all_gather(slot_rows, 'ctx', axis=0, tiled=True)  13.4 us
    sub x1, matrix products, shards(): scores - peak[:, :, None]  6.18 us
    dot_general x1, matrix products, shards(): jnp.dot(lnorm_all, qkv_weight[0, :, D:], preferred_element_type=jnp.float32)  3.76 us
    dot_general x1, matrix products, shards(): jnp.einsum('hqk,khe->hqe', weights.astype(jnp.bfloat16), values_part, pre...  3.31 us
    reduce_sum x2, other arithmetic, layer_norm(): spread = jnp.mean(center * center, axis=-1, keepdims=True)  2.95 us
  transfers between devices with their start and end apart: 1, of which 1 were waited for; matrix products, arithmetic and copies ran while one was open for 4% of the time, Pallas kernels for 0%

profile of v1, /device:TPU:1, one launch (start us, length us, event | category | flops | bytes accessed | tf_op | source)
XLA Modules:
  0.0 134.6 jit_solution(12979198201280572272)
XLA Ops:
  6.5 0.0 copy-start
  6.5 0.8 fusion.47
  7.3 0.2 convert_reduce_fusion.2
  7.5 1.3 reshape.64.ls_ref
  8.8 51.9 %encode.1 = bf16[32,768]{1,0:T(8,128)(2,1)} custom-call(bf16[32,16,16,384]{3,2,1,0:T(8,128)(2,1)} %x_ref.1, bf16[1536,768]{1,0:T(8,128)(2,1)} %down_ref.1, bf16[49,768]{1,0:T(8,128)(2,1)} %taps_ref.1, bf16[768,3072]{1,0:T(8,128)(2,1)} %w1_ref.1, bf16[3072,768]{1,0:T(8,128)(2,1)} %w2_ref.1, f32[1,768]{1,0:T(1,128)} %reshape.64.ls_ref), custom_call_target="tpu_custom_call" | custom-call | tf_op jit(solution)/shard_map/encode/pallas_call | solution.py:135
  60.7 0.1 broadcast_in_dim.29
  60.8 1.1 convolution_convert_fusion.1
  61.8 0.2 all_to_all.8
  62.0 24.3 %all_to_all.12 = bf16[128,2,896]{2,1,0:T(2,128)(2,1)S(1)} all-to-all(bf16[128,2,896]{2,1,0:T(2,128)(2,1)S(1)} %all_to_all.8), channel_id=1, replica_groups=mesh['slide'=32,'ctx'=4] {'slide','ctx'}, dimensions={0} | all-to-all | bytes 917504 | tf_op jit(solution)/shard_map/all_to_all | solution.py:189
  86.3 0.2 all_to_all.10
  86.5 0.1 add_reduce_fusion
  86.6 1.0 convert_reduce_fusion.1
  87.6 0.0 all-gather.2.cloned.1.call-update
  87.6 0.6 dynamic_slice.3
  88.3 0.6 add_compare_fusion
  88.9 0.6 iota_compare_fusion.5
  89.6 1.2 fusion.34
  90.8 1.8 %convolution_convert_fusion.2 = bf16[192,768]{1,0:T(8,128)(2,1)S(1)} fusion(bf16[1,768,2304]{2,1,0:T(8,128)(2,1)} %param.17, bf16[192,768]{1,0:T(8,128)(2,1)} %get-tuple-element.10, f32[192]{0:T(256)S(1)} %add_rsqrt_fusion.1, f32[192]{0:T(256)S(1)} %broadcast_multiply_fusion.1), kind=kOutput, calls=%fused_computation.24 | convolution fusion | flops 227229696 | bytes 1771008 | tf_op jit(solution)/shard_map/dot_general | solution.py:200
  92.6 0.9 copy.22
  93.5 13.4 %all-gather.2.cloned.1.call-done = bf16[768,768]{1,0:T(8,128)(2,1)} async-done(((bf16[192,768]{1,0:T(8,128)(2,1)}), bf16[768,768]{1,0:T(8,128)(2,1)}) %all-gather.2.cloned.1.call-update) | async-done | bytes 1179664 | tf_op jit(solution)/shard_map/all_gather | solution.py:194
  106.9 1.6 %convert_reduce_fusion = f32[768]{0:T(1024)S(1)} fusion(bf16[768,768]{1,0:T(8,128)(2,1)} %all-gather.2.cloned.1.call-done), kind=kLoop, calls=%fused_computation.11 | loop fusion | flops 1178880 | bytes 1182720 | tf_op jit(solution)/shard_map/reduce_sum | solution.py:168
  108.5 1.8 %fusion.9 = f32[768]{0:T(1024)S(1)} fusion(bf16[768,768]{1,0:T(8,128)(2,1)} %all-gather.2.cloned.1.call-done, f32[768]{0:T(1024)S(1)} %broadcast_multiply_fusion), kind=kLoop, calls=%fused_computation.14 | loop fusion | flops 2358528 | bytes 1185792 | tf_op jit(solution)/shard_map/reduce_sum | solution.py:169
  110.3 0.0 copy-done.1
  110.3 3.8 %convolution_convert_fusion = bf16[768,1536]{1,0:T(8,128)(2,1)S(1)} fusion(bf16[1,768,2304]{2,1,0:T(8,128)(2,1)} %param.17, bf16[768,768]{1,0:T(8,128)(2,1)S(1)} %copy-done.1, f32[768]{0:T(1024)S(1)} %add_rsqrt_fusion, f32[768]{0:T(1024)S(1)} %broadcast_multiply_fusion), kind=kOutput, calls=%fused_computation.9 | convolution fusion | flops 1815478272 | bytes 5904384 | tf_op jit(solution)/shard_map/dot_general | solution.py:202
  114.1 0.2 fusion.52
  114.2 1.4 %copy.23 = bf16[768,768]{0,1:T(8,128)(2,1)} copy(bf16[768,768]{1,0:T(8,128)(2,1)S(1)} %get-tuple-element.5) | data formatting | bytes 2359296 | tf_op jit(solution)/shard_map/slice | solution.py:204
  115.7 1.4 %copy.24 = bf16[768,768]{0,1:T(8,128)(2,1)} copy(bf16[768,768]{1,0:T(8,128)(2,1)S(1)} %get-tuple-element.6) | data formatting | bytes 2359296 | tf_op jit(solution)/shard_map/slice | solution.py:205
  117.1 6.2 %fusion.53 = (f32[12,192]{1,0:T(8,128)}, bf16[12,192,768]{2,1,0:T(8,128)(2,1)}) fusion(pred[768]{0:T(1024)(128)(4,1)S(1)} %iota_compare_fusion.5, bf16[192,12,64]{0,2,1:T(8,128)(2,1)} %bitcast.30, bf16[768,12,64]{0,2,1:T(8,128)(2,1)S(1)} %bitcast.28), kind=kOutput, calls=%fused_computation.69 | convolution fusion | flops 237110016 | bytes 5023488 | tf_op jit(solution)/shard_map/sub | solution.py:210
  123.3 0.0 copy-done.3
  123.3 3.3 %fusion.19 = bf16[192,12,64]{0,2,1:T(8,128)(2,1)S(1)} fusion(bf16[768,12,64]{0,2,1:T(8,128)(2,1)S(1)} %bitcast.29, bf16[12,192,768]{2,1,0:T(8,128)(2,1)} %get-tuple-element.12, f32[192,12]{0,1:T(8,128)} %bitcast.32), kind=kOutput, calls=%fused_computation.22 | convolution fusion | flops 226787328 | bytes 5022720 | tf_op jit(solution)/shard_map/hqk,khe->hqe/dot_general | solution.py:212
  126.6 0.0 copy-done.4
  126.6 1.1 fusion.23
  (14 shorter events, 0.0 us)
Async XLA Ops:
  6.5 120.1 %copy-start = (bf16[1,768,768]{2,1,0:T(8,128)(2,1)S(1)}, bf16[1,768,768]{2,1,0:T(8,128)(2,1)}, u32[]{:S(2)}) copy-start(bf16[1,768,768]{2,1,0:T(8,128)(2,1)} %param.18) | copy-start | bytes 3538948
  6.5 100.4 %all-gather.2.cloned.1.call-start = ((), (), s32[]{:S(2)}) async-start(), calls=%async_computation.1 | async-start | bytes 1474560 | tf_op jit(solution)/shard_map/all_gather | solution.py:194
  60.7 26.9 %copy-start.5 = (s32[32]{0:T(128)S(1)}, s32[32]{0:T(128)}, u32[]{:S(2)}) copy-start(s32[32]{0:T(128)} %param.21) | copy-start | bytes 388
  106.9 3.4 %copy-start.1 = (bf16[768,768]{1,0:T(8,128)(2,1)S(1)}, bf16[768,768]{1,0:T(8,128)(2,1)}, u32[]{:S(2)}) copy-start(bf16[768,768]{1,0:T(8,128)(2,1)} %all-gather.2.cloned.1.call-done) | copy-start | bytes 3538948
  115.7 1.4 %copy-start.2 = (bf16[768,768]{0,1:T(8,128)(2,1)S(1)}, bf16[768,768]{0,1:T(8,128)(2,1)}, u32[]{:S(2)}) copy-start(bf16[768,768]{0,1:T(8,128)(2,1)} %copy.23) | copy-start | bytes 3538948
  117.1 6.2 %copy-start.3 = (bf16[768,768]{0,1:T(8,128)(2,1)S(1)}, bf16[768,768]{0,1:T(8,128)(2,1)}, u32[]{:S(2)}) copy-start(bf16[768,768]{0,1:T(8,128)(2,1)} %copy.24) | copy-start | bytes 3538948
  123.3 3.3 %copy-start.4 = (bf16[192,768]{1,0:T(8,128)(2,1)S(1)}, bf16[192,768]{1,0:T(8,128)(2,1)}, u32[]{:S(2)}) copy-start(bf16[192,768]{1,0:T(8,128)(2,1)} %get-tuple-element.10) | copy-start | bytes 884740
Sparse Core Ops, SparseCore 0:
  87.7 19.1 all-gather.1

commit v2 on v1

--- a/solution.py
+++ b/solution.py
@@ -161,58 +161,172 @@
 HEADS = 12
 HEAD_DIM = 64
 SEQ_DEV = 192
+HALF_SEQ = 96
+CAP = 2
+CODED = D + 128
 FAR_NEGATIVE = -1e30
-
-
-def layer_norm(values):
-    center = values - jnp.mean(values, axis=-1, keepdims=True)
-    spread = jnp.mean(center * center, axis=-1, keepdims=True)
+MESH = pl.DeviceIdType.MESH
+
+
+def row_norm(values):
+    center = values - jnp.sum(values, axis=-1, keepdims=True) * (1.0 / D)
+    spread = jnp.sum(center * center, axis=-1, keepdims=True) * (1.0 / D)
     return center * lax.rsqrt(spread + NORM_EPS)
+
+
+def route_kernel(slides, ctxs, out_ref, rows_ref, recv_ref, a2a_send, a2a_recv, own_sem, ring_send, ring_recv):
+    count = slides * ctxs
+    slide = lax.axis_index("slide")
+    ctx = lax.axis_index("ctx")
+    me = slide * ctxs + ctx
+    barrier = pltpu.get_barrier_semaphore()
+
+    def greet(k, _):
+        peer = lax.rem(me + k, count)
+        pl.semaphore_signal(barrier, inc=1, device_id=(peer // ctxs, lax.rem(peer, ctxs)), device_id_type=MESH)
+        return 0
+    lax.fori_loop(1, count, greet, 0)
+    pl.semaphore_wait(barrier, count - 1)
+
+    own = pltpu.make_async_copy(out_ref.at[me], recv_ref.at[me], own_sem)
+    own.start()
+
+    def send(k, _):
+        peer = lax.rem(me + k, count)
+        pltpu.make_async_remote_copy(
+            src_ref=out_ref.at[peer], dst_ref=recv_ref.at[me], send_sem=a2a_send, recv_sem=a2a_recv,
+            device_id=(peer // ctxs, lax.rem(peer, ctxs)), device_id_type=MESH).start()
+        return 0
+    lax.fori_loop(1, count, send, 0)
+    own.wait()
+    rest = pl.ds(0, count - 1)
+    whole = pltpu.make_async_remote_copy(
+        src_ref=out_ref.at[rest], dst_ref=recv_ref.at[rest], send_sem=a2a_send, recv_sem=a2a_recv,
+        device_id=(slide, ctx), device_id_type=MESH)
+    whole.wait_recv()
+
+    arrived = recv_ref[...].reshape(count * CAP, CODED)
+    code = arrived[:, D:].astype(jnp.float32)
+    lane = lax.broadcasted_iota(jnp.int32, (count * CAP, 128), 1).astype(jnp.float32) + 1.0
+    pick = jnp.concatenate([jnp.where(code == lane, 1.0, 0.0), jnp.where(code == lane + 128.0, 1.0, 0.0)], axis=1)
+    mine = lax.dot_general(pick.astype(jnp.bfloat16), arrived[:, :D], (((0,), (0,)), ((), ())),
+                           preferred_element_type=jnp.float32)
+    rows_ref[ctx] = mine[:SEQ_DEV].astype(jnp.bfloat16)
+
+    right = lax.rem(ctx + 1, ctxs)
+    left = lax.rem(ctx + ctxs - 1, ctxs)
+    first, second = pl.ds(0, HALF_SEQ), pl.ds(HALF_SEQ, HALF_SEQ)
+
+    def hop(n, block, half, to):
+        return pltpu.make_async_remote_copy(
+            src_ref=rows_ref.at[block, half], dst_ref=rows_ref.at[block, half],
+            send_sem=ring_send.at[n], recv_sem=ring_recv.at[n], device_id=(slide, to), device_id_type=MESH)
+    own_hops = [hop(0, ctx, first, right), hop(1, ctx, second, left), hop(2, ctx, second, right), hop(3, ctx, first, left)]
+    for h in own_hops:
+        h.start()
+    own_hops[0].wait_recv()
+    onward = hop(4, left, first, right)
+    onward.start()
+    own_hops[1].wait_recv()
+    back = hop(5, right, second, left)
+    back.start()
+    own_hops[2].wait_recv()
+    own_hops[3].wait_recv()
+    onward.wait_recv()
+    back.wait_recv()
+    for h in own_hops + [onward, back]:
+        h.wait_send()
+    whole.wait_send()
+
+
+def route(outgoing, slides, ctxs):
+    import functools
+    count = slides * ctxs
+    return pl.pallas_call(
+        functools.partial(route_kernel, slides, ctxs),
+        out_shape=jax.ShapeDtypeStruct((ctxs, SEQ_DEV, D), jnp.bfloat16),
+        in_specs=[pl.BlockSpec(memory_space=pltpu.VMEM)],
+        out_specs=pl.BlockSpec(memory_space=pltpu.VMEM),
+        scratch_shapes=[
+            pltpu.VMEM((count, CAP, CODED), jnp.bfloat16),
+            pltpu.SemaphoreType.DMA, pltpu.SemaphoreType.DMA, pltpu.SemaphoreType.DMA,
+            pltpu.SemaphoreType.DMA((6,)), pltpu.SemaphoreType.DMA((6,)),
+        ],
+        compiler_params=pltpu.CompilerParams(collective_id=0, has_side_effects=True),
+        name="route",
+    )(outgoing)
+
+
+def attend_kernel(where_ref, rows_ref, wqkv_ref, wout_ref, out_ref, ln_ref, k_ref, v_ref, q_ref, att_ref):
+    length = where_ref[0]
+    ctx = where_ref[1]
+    total = k_ref.shape[0]
+
+    def norm(n, _):
+        base = pl.multiple_of(n * 64, 64)
+        ln_ref[pl.ds(base, 64), :] = row_norm(rows_ref[pl.ds(base, 64), :].astype(jnp.float32)).astype(jnp.bfloat16)
+        return 0
+    lax.fori_loop(0, total // 64, norm, 0, unroll=3)
+    start = pl.multiple_of(ctx * SEQ_DEV, 64)
+    q = jnp.dot(ln_ref[pl.ds(start, SEQ_DEV), :], wqkv_ref[:, :D], preferred_element_type=jnp.float32)
+    q_ref[...] = (q.astype(jnp.bfloat16).astype(jnp.float32) * HEAD_DIM ** (-0.5)).astype(jnp.bfloat16)
+    k_ref[...] = jnp.dot(ln_ref[...], wqkv_ref[:, D:2 * D], preferred_element_type=jnp.float32).astype(jnp.bfloat16)
+    v_ref[...] = jnp.dot(ln_ref[...], wqkv_ref[:, 2 * D:], preferred_element_type=jnp.float32).astype(jnp.bfloat16)
+    key = lax.broadcasted_iota(jnp.int32, (1, total), 1)
+    bias = jnp.where(key < length, 0.0, FAR_NEGATIVE)
+    low = lax.broadcasted_iota(jnp.int32, (SEQ_DEV, 128), 1) < HEAD_DIM
+    for pair in range(HEADS // 2):
+        cols = slice(pair * 128, pair * 128 + 128)
+        q2 = q_ref[:, cols]
+        zero = jnp.zeros_like(q2)
+        both = jnp.concatenate([jnp.where(low, q2, zero), jnp.where(low, zero, q2)], axis=0)
+        s = lax.dot_general(both, k_ref[:, cols], (((1,), (1,)), ((), ())), preferred_element_type=jnp.float32) + bias
+        w = jnp.exp(s - jnp.max(s, axis=-1, keepdims=True))
+        denom = jnp.sum(w, axis=-1, keepdims=True)
+        o = jnp.dot(w.astype(jnp.bfloat16), v_ref[:, cols], preferred_element_type=jnp.float32) / denom
+        att_ref[:, cols] = jnp.where(low, o[:SEQ_DEV], o[SEQ_DEV:]).astype(jnp.bfloat16)
+    out = jnp.dot(att_ref[...], wout_ref[...], preferred_element_type=jnp.float32)
+    out = out + rows_ref[pl.ds(start, SEQ_DEV), :].astype(jnp.float32)
+    row = lax.broadcasted_iota(jnp.int32, (SEQ_DEV, 1), 0) + start
+    out_ref[...] = jnp.where(row < length, out, 0.0).astype(jnp.bfloat16)
+
+
+def attend(where, rows, wqkv, wout):
+    total = rows.shape[0]
+    vmem = pl.BlockSpec(memory_space=pltpu.VMEM)
+    return pl.pallas_call(
+        attend_kernel,
+        out_shape=jax.ShapeDtypeStruct((SEQ_DEV, D), jnp.bfloat16),
+        in_specs=[pl.BlockSpec(memory_space=pltpu.SMEM), vmem, vmem, vmem],
+        out_specs=vmem,
+        scratch_shapes=[
+            pltpu.VMEM((total, D), jnp.bfloat16), pltpu.VMEM((total, D), jnp.bfloat16),
+            pltpu.VMEM((total, D), jnp.bfloat16), pltpu.VMEM((SEQ_DEV, D), jnp.bfloat16),
+            pltpu.VMEM((SEQ_DEV, D), jnp.bfloat16),
+        ],
+        compiler_params=pltpu.CompilerParams(vmem_limit_bytes=40 << 20),
+        name="attend",
+    )(where, rows, wqkv, wout)
 
 
 def shards(feature_maps, down_weight, conv_taps, mlp_in, mlp_out, layer_scale, qkv_weight, out_weight,
            tile_slide, tile_pos, slide_len):
-    ctx_count = lax.axis_size("ctx")
-    device_count = lax.axis_size("slide") * ctx_count
-    capacity = (SEQ_DEV + device_count - 1) // device_count
+    ctxs = lax.axis_size("ctx")
+    slides = lax.axis_size("slide")
     tiles_here = feature_maps.shape[0]
     embeds = encode_tiles(feature_maps, down_weight, conv_taps, mlp_in, mlp_out, layer_scale)
-    owner_index = tile_slide * ctx_count + tile_pos // SEQ_DEV
+    owner_index = tile_slide * ctxs + tile_pos // SEQ_DEV
     tile_order = jnp.arange(tiles_here, dtype=jnp.int32)
     earlier = (owner_index[None, :] == owner_index[:, None]) & (tile_order[None, :] < tile_order[:, None])
     tile_rank = jnp.sum(earlier.astype(jnp.int32), axis=1)
-    target_row = owner_index * capacity + tile_rank
-    placing = jnp.arange(device_count * capacity, dtype=jnp.int32)[:, None] == target_row[None, :]
+    target_row = owner_index * CAP + tile_rank
+    placing = jnp.arange(slides * ctxs * CAP, dtype=jnp.int32)[:, None] == target_row[None, :]
     slot_code = (tile_pos % SEQ_DEV + 1).astype(jnp.bfloat16)
     coded = jnp.concatenate([embeds, jnp.broadcast_to(slot_code[:, None], (tiles_here, 128))], axis=1)
     outgoing = jnp.dot(placing.astype(jnp.bfloat16), coded, preferred_element_type=jnp.float32).astype(jnp.bfloat16)
-    arrived = lax.all_to_all(outgoing, ("slide", "ctx"), split_axis=0, concat_axis=0, tiled=True)
-    arrived_slot = arrived[:, D].astype(jnp.int32) - 1
-    position = jnp.arange(SEQ_DEV, dtype=jnp.int32)
-    picking = (position[:, None] == arrived_slot[None, :]).astype(jnp.bfloat16)
-    slot_rows = jnp.dot(picking, arrived[:, :D], preferred_element_type=jnp.float32).astype(jnp.bfloat16)
-    all_rows = lax.all_gather(slot_rows, "ctx", axis=0, tiled=True)
-    length = slide_len[lax.axis_index("slide")]
-    query_pos = lax.axis_index("ctx") * SEQ_DEV + position
-    stream = slot_rows.astype(jnp.float32)
-    lnorm = layer_norm(stream).astype(jnp.bfloat16)
-    lnorm_all = layer_norm(all_rows.astype(jnp.float32)).astype(jnp.bfloat16)
-    queries = jnp.dot(lnorm, qkv_weight[0, :, :D], preferred_element_type=jnp.float32).astype(jnp.bfloat16)
-    queries = queries.reshape(SEQ_DEV, HEADS, HEAD_DIM)
-    key_rows = jnp.dot(lnorm_all, qkv_weight[0, :, D:], preferred_element_type=jnp.float32).astype(jnp.bfloat16)
-    row_count = key_rows.shape[0]
-    keys_part = key_rows[:, :D].reshape(row_count, HEADS, HEAD_DIM)
-    values_part = key_rows[:, D:].reshape(row_count, HEADS, HEAD_DIM)
-    scores = jnp.einsum("qhe,khe->hqk", queries, keys_part, preferred_element_type=jnp.float32) * HEAD_DIM ** (-0.5)
-    included = jnp.arange(row_count, dtype=jnp.int32) < length
-    scores = jnp.where(included[None, None, :], scores, FAR_NEGATIVE)
-    peak = jnp.max(scores, axis=-1)
-    weights = jnp.where(included[None, None, :], jnp.exp(scores - peak[:, :, None]), 0.0)
-    denom_sum = jnp.sum(weights, axis=-1)
-    accum = jnp.einsum("hqk,khe->hqe", weights.astype(jnp.bfloat16), values_part, preferred_element_type=jnp.float32)
-    attended = (accum / denom_sum[:, :, None]).transpose(1, 0, 2).reshape(SEQ_DEV, D).astype(jnp.bfloat16)
-    stream = stream + jnp.dot(attended, out_weight[0], preferred_element_type=jnp.float32)
-    return jnp.where((query_pos < length)[:, None], stream, 0.0).astype(jnp.bfloat16)
+    rows = route(outgoing.reshape(slides * ctxs, CAP, CODED), slides, ctxs).reshape(ctxs * SEQ_DEV, D)
+    where = jnp.stack([slide_len[lax.axis_index("slide")], lax.axis_index("ctx")])
+    return attend(where, rows, qkv_weight[0], out_weight[0])
 
 
 def solution(mesh):

time: 135 us -> 104 us (0.77)
  Pallas kernels: 51.9 us -> 92.7 us
  blocking collectives: 24.3 us -> 0 us
  matrix products: 18.2 us -> 1.82 us
  between operations: 13.5 us -> 0.03 us
  waiting for transfers between devices: 13.4 us -> 0 us
  other arithmetic: 6.88 us -> 1.58 us
    pallas_call x0 -> x2, Pallas kernels: none -> 40.7 us  [the longest x1 33.5 us: route(): pl.pallas_call(functools.partial(route_kernel, slides, ctxs), out_shape=j...]
    all_to_all x1 -> x0, blocking collectives: 24.3 us -> none  [shards(): lax.all_to_all(outgoing, ('slide', 'ctx'), split_axis=0, concat_axis=0, t...]
    all_gather x1 -> x0, waiting for transfers between devices: 13.4 us -> none  [shards(): all_rows = lax.all_gather(slot_rows, 'ctx', axis=0, tiled=True)]
    dot_general x5 -> x0, matrix products: 11 us -> none  [the longest x1 3.76 us: shards(): jnp.dot(lnorm_all, qkv_weight[0, :, D:], preferred_element_type=jnp.float32)]
    sub x1 -> x0, matrix products: 6.18 us -> none  [shards(): scores - peak[:, :, None]]
    reduce_sum x3 -> x0, other arithmetic: 4.54 us -> none  [the longest x2 2.95 us: layer_norm(): spread = jnp.mean(center * center, axis=-1, keepdims=True)]
    slice x3 -> x0, local copies, waits for them, and re-layouts: 3.04 us -> none  [the longest x2 1.6 us: shards(): keys_part = key_rows[:, :D].reshape(row_count, HEADS, HEAD_DIM)]
    unnamed x12 -> x6, local copies, waits for them, and re-layouts: 0.02 us -> 2.54 us
  transfers between devices with their start and end apart: 1 -> 0, of which waited for: 1 -> 0; matrix products, arithmetic and copies ran while one was open for 4% -> 0% of each run, Pallas kernels for 0% -> 0%
where the time goes in v2:
time: 104 us; the launch traced here: 103 us
  Pallas kernels  92.7 us (89%)
  local copies, waits for them, and re-layouts  7.11 us (7%)
  matrix products  1.82 us (2%)
  other arithmetic  1.58 us (2%)
    pallas_call x1, Pallas kernels, encode_tiles(): pl.pallas_call(encode_kernel, out_shape=jax.ShapeDtypeStruct((nt, D), jnp...  52 us
    pallas_call x1, Pallas kernels, route(): pl.pallas_call(functools.partial(route_kernel, slides, ctxs), out_shape=j...  33.5 us
    pallas_call x1, Pallas kernels, attend(): pl.pallas_call(attend_kernel, out_shape=jax.ShapeDtypeStruct((SEQ_DEV, D)...  7.19 us
    unnamed x6, local copies, waits for them, and re-layouts  2.54 us

profile of v2, /device:TPU:1, one launch (start us, length us, event | category | flops | bytes accessed | tf_op | source)
XLA Modules:
  0.0 103.3 jit_solution(1007678449056964881)
XLA Ops:
  0.0 1.3 %dynamic_slice.3 = s32[1]{0:T(128)} dynamic-slice(s32[32]{0:T(128)} %param.21, s32[]{:T(128)S(6)} %select_n.15), dynamic_slice_sizes={1} | dynamic-slice | bytes 12 | tf_op jit(solution)/shard_map/dynamic_slice | solution.py:328
  1.3 0.7 pad_add_fusion.where_ref
  2.0 0.7 fusion.6
  2.7 0.2 convert_reduce_fusion
  2.8 1.3 %reshape.13.ls_ref = f32[1,768]{1,0:T(1,128)} reshape(f32[768]{0:T(1024)} %param.16) | data formatting | bytes 6144 | tf_op jit(solution)/shard_map/reshape | solution.py:156
  4.1 0.1 broadcast_in_dim.2
  4.2 0.0 copy-start.1
  4.2 52.0 %encode.1 = bf16[32,768]{1,0:T(8,128)(2,1)} custom-call(bf16[32,16,16,384]{3,2,1,0:T(8,128)(2,1)} %x_ref.1, bf16[1536,768]{1,0:T(8,128)(2,1)} %down_ref.1, bf16[49,768]{1,0:T(8,128)(2,1)} %taps_ref.1, bf16[768,3072]{1,0:T(8,128)(2,1)} %w1_ref.1, bf16[3072,768]{1,0:T(8,128)(2,1)} %w2_ref.1, f32[1,768]{1,0:T(1,128)} %reshape.13.ls_ref), custom_call_target="tpu_custom_call" | custom-call | tf_op jit(solution)/shard_map/encode/pallas_call | solution.py:135
  56.2 1.8 %convolution_convert_fusion = bf16[256,896]{1,0:T(8,128)(2,1)} fusion(s32[32]{0:T(128)S(1)} %multiply_add_fusion, bf16[32,128]{1,0:T(8,128)(2,1)S(1)} %broadcast_in_dim.2, bf16[32,768]{1,0:T(8,128)(2,1)} %encode.1), kind=kOutput, calls=%fused_computation | convolution fusion | flops 15032320 | bytes 516224 | tf_op jit(solution)/shard_map/dot_general | solution.py:326
  58.0 2.0 %reshape.14.out_ref = bf16[128,2,896]{2,1,0:T(2,128)(2,1)} reshape(bf16[256,896]{1,0:T(8,128)(2,1)} %convolution_convert_fusion) | data formatting | bytes 917504 | tf_op jit(solution)/shard_map/reshape | solution.py:327
  60.0 33.5 %route.1 = bf16[4,192,768]{2,1,0:T(8,128)(2,1)} custom-call(bf16[128,2,896]{2,1,0:T(2,128)(2,1)} %reshape.14.out_ref), custom_call_target="tpu_custom_call" | custom-call | tf_op jit(solution)/shard_map/route/pallas_call | solution.py:245
  93.5 0.0 copy-done.1
  93.5 0.0 copy-start
  93.5 1.3 %copy-done = bf16[4,192,768]{2,1,0:T(8,128)(2,1)S(1)} copy-done((bf16[4,192,768]{2,1,0:T(8,128)(2,1)S(1)}, bf16[4,192,768]{2,1,0:T(8,128)(2,1)}, u32[]{:S(2)}) %copy-start) | copy-done | bytes 1179672
  94.8 0.0 copy-start.2
  94.8 1.3 %copy-done.2 = bf16[1,768,768]{2,1,0:T(8,128)(2,1)S(1)} copy-done((bf16[1,768,768]{2,1,0:T(8,128)(2,1)S(1)}, bf16[1,768,768]{2,1,0:T(8,128)(2,1)}, u32[]{:S(2)}) %copy-start.2) | copy-done | bytes 1179672
  96.1 7.2 %attend.1 = bf16[192,768]{1,0:T(8,128)(2,1)} custom-call(s32[2]{0:T(128)S(1)} %pad_add_fusion.where_ref, bf16[768,768]{1,0:T(8,128)(2,1)S(1)} %bitcast.4, bf16[768,2304]{1,0:T(8,128)(2,1)S(1)} %bitcast.5, bf16[768,768]{1,0:T(8,128)(2,1)S(1)} %bitcast.6), custom_call_target="tpu_custom_call" | custom-call | tf_op jit(solution)/shard_map/attend/pallas_call | solution.py:297
  (1 shorter events, 0.0 us)
Async XLA Ops:
  4.2 89.3 %copy-start.1 = (bf16[1,768,2304]{2,1,0:T(8,128)(2,1)S(1)}, bf16[1,768,2304]{2,1,0:T(8,128)(2,1)}, u32[]{:S(2)}) copy-start(bf16[1,768,2304]{2,1,0:T(8,128)(2,1)} %param.17) | copy-start | bytes 10616836
  93.5 1.3 %copy-start = (bf16[4,192,768]{2,1,0:T(8,128)(2,1)S(1)}, bf16[4,192,768]{2,1,0:T(8,128)(2,1)}, u32[]{:S(2)}) copy-start(bf16[4,192,768]{2,1,0:T(8,128)(2,1)} %route.1) | copy-start | bytes 3538948
  94.8 1.3 %copy-start.2 = (bf16[1,768,768]{2,1,0:T(8,128)(2,1)S(1)}, bf16[1,768,768]{2,1,0:T(8,128)(2,1)}, u32[]{:S(2)}) copy-start(bf16[1,768,768]{2,1,0:T(8,128)(2,1)} %param.18) | copy-start | bytes 3538948

commit v3 on v2

v3 whole, which is shorter than its diff:
```python
import functools

import jax
import jax.numpy as jnp
from jax import lax
from jax.experimental import pallas as pl
from jax.experimental.pallas import tpu as pltpu

NORM_EPS = 1e-06
GROUP = 8
HALF = 8
KS = 7
C_IN = 384
D = 768
LB = D // 128
MLP = 3072
HC = 512
PITCH = 257
INV_SQRT2 = 0.7071067811865476


def split_bf16(values):
    high = values.astype(jnp.bfloat16)
    return high, (values - high.astype(jnp.float32)).astype(jnp.bfloat16)


def lane_total(values, ones):
    return jnp.dot(jnp.concatenate(split_bf16(values), axis=-1), ones, preferred_element_type=jnp.float32)


def norm_maps(x_ref, s_ref, g):
    ones = jnp.full((256, 128), 1.0, jnp.bfloat16)
    inv_n = 1.0 / C_IN

    def one_tile(t, _):
        def parts():
            x = x_ref[g * GROUP + t].reshape(256, C_IN)
            return [x[:, l * 128:(l + 1) * 128].astype(jnp.float32) for l in range(3)]
        xs = parts()
        mean = lane_total(xs[0] + xs[1] + xs[2], ones) * inv_n
        cs = [x - mean for x in xs]
        var = lane_total(cs[0] * cs[0] + cs[1] * cs[1] + cs[2] * cs[2], ones) * inv_n
        inv = lax.rsqrt(var + NORM_EPS)
        for l in range(3):
            s_ref[l, pl.ds(t * PITCH, 256), :] = cs[l] * inv
        return 0

    lax.fori_loop(0, GROUP, one_tile, 0, unroll=2)


def make_patches(s_ref, l_ref):
    def patch_rows(n, _):
        i = n // 4
        jp = (n % 4) * 2
        row = pl.multiple_of((i * HALF + jp) * GROUP, 16)
        for dy in range(2):
            for dx in range(2):
                for l in range(3):
                    pos = (2 * i + dy) * 16 + 2 * jp + dx
                    a = s_ref[l, pl.ds(pos, GROUP, stride=PITCH), :]
                    b = s_ref[l, pl.ds(pos + 2, GROUP, stride=PITCH), :]
                    col = (dy * 2 + dx) * C_IN + l * 128
                    l_ref[pl.ds(row, 16), col:col + 128] = jnp.concatenate([a, b], axis=0).astype(jnp.bfloat16)
        return 0
    lax.fori_loop(0, HALF * HALF // 2, patch_rows, 0, unroll=2)


def reduce_chunk(n, l_ref, down_ref, r_ref):
    cols = pl.ds(pl.multiple_of(n * 256, 256), 256)
    red = jnp.dot(l_ref[...], down_ref[:, cols], preferred_element_type=jnp.float32)
    red = red.astype(jnp.bfloat16).astype(jnp.float32)
    for h in range(2):
        r_ref[n * 2 + h] = red[:, h * 128:(h + 1) * 128].reshape(64, GROUP, 128)


def conv_lane(l, r_ref, tap_ref, sp_ref, pr_ref, g):
    psum = None
    for i in range(HALF):
        acc = [None] * HALF
        for a in range(KS):
            ii = i + a - 3
            if not 0 <= ii < HALF:
                continue
            xs = [r_ref[l, ii * HALF + j] for j in range(HALF)]
            for b in range(KS):
                w = tap_ref[l, a * KS + b]
                for j in range(HALF):
                    jj = j + b - 3
                    if 0 <= jj < HALF:
                        term = xs[jj] * w
                        acc[j] = term if acc[j] is None else acc[j] + term
            if ii == i:
                row = ((xs[0] + xs[1]) + (xs[2] + xs[3])) + ((xs[4] + xs[5]) + (xs[6] + xs[7]))
                psum = row if psum is None else psum + row
        for j in range(HALF):
            sp_ref[l, i * HALF + j] = acc[j]
    pr_ref[l, g * GROUP:(g + 1) * GROUP, :] = psum


def norm_spatial(sp_ref, sn_ref):
    def some_rows(n, _):
        rows = [sp_ref[l, pl.ds(n * 8, 8)].reshape(64, 128) for l in range(LB)]
        tot = ((rows[0] + rows[1]) + (rows[2] + rows[3])) + (rows[4] + rows[5])
        mean = jnp.sum(tot, axis=-1, keepdims=True) * (1.0 / D)
        cs = [r - mean for r in rows]
        sq = [c * c for c in cs]
        sq = ((sq[0] + sq[1]) + (sq[2] + sq[3])) + (sq[4] + sq[5])
        inv = lax.rsqrt(jnp.sum(sq, axis=-1, keepdims=True) * (1.0 / D) + NORM_EPS)
        for l in range(LB):
            sn_ref[pl.ds(pl.multiple_of(n * 64, 64), 64), l * 128:(l + 1) * 128] = (cs[l] * inv).astype(jnp.bfloat16)
        return 0
    lax.fori_loop(0, 8, some_rows, 0, unroll=4)


def hidden_chunk(c, sn_ref, w1_ref, ph_ref, g):
    cols = pl.ds(pl.multiple_of(c * HC, HC), HC)
    h = jnp.dot(sn_ref[...], w1_ref[:, cols], preferred_element_type=jnp.float32)
    h = h + h * lax.erf(h * INV_SQRT2)
    ph_ref[g * GROUP:(g + 1) * GROUP, cols] = jnp.sum(h.reshape(64, GROUP, HC), axis=0)


def encode_kernel(groups, x_hbm, down_hbm, taps_ref, w1_hbm, w2_hbm, ls_ref, out_ref,
                  x_ref, down_ref, w1_ref, w2_ref, s_ref, l0_ref, l1_ref, r0_ref, r1_ref, sp_ref, sn_ref, tap_ref, ph_ref, pr_ref, sems):
    l_bufs, r_bufs = (l0_ref, l1_ref), (r0_ref, r1_ref)
    x_copy = [pltpu.make_async_copy(x_hbm.at[pl.ds(g * GROUP, GROUP)], x_ref.at[pl.ds(g * GROUP, GROUP)], sems.at[g])
              for g in range(groups)]
    down_copy = pltpu.make_async_copy(down_hbm, down_ref, sems.at[groups])
    w1_copy = pltpu.make_async_copy(w1_hbm, w1_ref, sems.at[groups + 1])
    w2_copy = pltpu.make_async_copy(w2_hbm, w2_ref, sems.at[groups + 2])
    x_copy[0].start()
    down_copy.start()
    t = taps_ref[...].astype(jnp.float32)
    for k in range(KS * KS):
        for l in range(LB):
            tap_ref[l, k] = jnp.broadcast_to(t[k:k + 1, l * 128:(l + 1) * 128], (8, 128))
    x_copy[0].wait()
    x_copy[1].start()
    w1_copy.start()
    norm_maps(x_ref, s_ref, 0)
    make_patches(s_ref, l0_ref)
    for g in range(2, groups):
        x_copy[g].start()
    w2_copy.start()
    down_copy.wait()

    def first(n, _):
        reduce_chunk(n, l0_ref, down_ref, r0_ref)
        return 0
    lax.fori_loop(0, 3, first, 0)
    x_copy[1].wait()
    norm_maps(x_ref, s_ref, 1)
    make_patches(s_ref, l1_ref)

    for g in range(groups + 1):
        if g == 1:
            w1_copy.wait()

        def step(n, _):
            if g >= 1:
                hidden_chunk(2 * n, sn_ref, w1_ref, ph_ref, g - 1)
            if g < groups:
                conv_lane(2 * n, r_bufs[g % 2], tap_ref, sp_ref, pr_ref, g)
            if g >= 1:
                hidden_chunk(2 * n + 1, sn_ref, w1_ref, ph_ref, g - 1)
            if g < groups:
                conv_lane(2 * n + 1, r_bufs[g % 2], tap_ref, sp_ref, pr_ref, g)
            if g + 1 < groups:
                reduce_chunk(n, l_bufs[(g + 1) % 2], down_ref, r_bufs[(g + 1) % 2])
            return 0
        lax.fori_loop(0, 3, step, 0)
        if g < groups:
            norm_spatial(sp_ref, sn_ref)
        if g + 2 < groups:
            x_copy[g + 2].wait()
            norm_maps(x_ref, s_ref, g + 2)
            make_patches(s_ref, l_bufs[g % 2])

    w2_copy.wait()
    br = jnp.dot(jnp.concatenate(split_bf16(ph_ref[...]), axis=0), w2_ref[...], preferred_element_type=jnp.float32)
    nt = groups * GROUP
    br = br[:nt] + br[nt:]
    pr = jnp.concatenate([pr_ref[l] for l in range(LB)], axis=-1)
    pooled = (pr + ls_ref[...].reshape(1, D) * (0.5 * br)) * (1.0 / (HALF * HALF))
    c = pooled - jnp.mean(pooled, axis=-1, keepdims=True)
    v = jnp.mean(c * c, axis=-1, keepdims=True)
    out_ref[...] = (c * lax.rsqrt(v + NORM_EPS)).astype(jnp.bfloat16)


def encode_tiles(x, down, taps, w1, w2, ls):
    nt = x.shape[0]
    groups = nt // GROUP
    hbm = pl.BlockSpec(memory_space=pl.ANY)
    vmem = pl.BlockSpec(memory_space=pltpu.VMEM)
    return pl.pallas_call(
        functools.partial(encode_kernel, groups),
        out_shape=jax.ShapeDtypeStruct((nt, D), jnp.bfloat16),
        in_specs=[hbm, hbm, vmem, hbm, hbm, vmem],
        out_specs=vmem,
        scratch_shapes=[
            pltpu.VMEM((nt, 16, 16, C_IN), jnp.bfloat16),
            pltpu.VMEM((4 * C_IN, D), jnp.bfloat16),
            pltpu.VMEM((D, MLP), jnp.bfloat16),
            pltpu.VMEM((MLP, D), jnp.bfloat16),
            pltpu.VMEM((3, GROUP * PITCH, 128), jnp.float32),
            pltpu.VMEM((64 * GROUP, 4 * C_IN), jnp.bfloat16),
            pltpu.VMEM((64 * GROUP, 4 * C_IN), jnp.bfloat16),
            pltpu.VMEM((LB, 64, GROUP, 128), jnp.float32),
            pltpu.VMEM((LB, 64, GROUP, 128), jnp.float32),
            pltpu.VMEM((LB, 64, GROUP, 128), jnp.float32),
            pltpu.VMEM((64 * GROUP, D), jnp.bfloat16),
            pltpu.VMEM((LB, KS * KS, 8, 128), jnp.float32),
            pltpu.VMEM((nt, MLP), jnp.float32),
            pltpu.VMEM((LB, nt, 128), jnp.float32),
            pltpu.SemaphoreType.DMA((groups + 3,)),
        ],
        compiler_params=pltpu.CompilerParams(vmem_limit_bytes=56 << 20),
        name="encode",
    )(x, down, taps, w1, w2, ls)


from jax.sharding import PartitionSpec as P

HEADS = 12
HEAD_DIM = 64
SEQ_DEV = 192
HALF_SEQ = 96
CAP = 2
CODED = D + 128
FAR_NEGATIVE = -1e30
MESH = pl.DeviceIdType.MESH


def row_norm(values):
    center = values - jnp.sum(values, axis=-1, keepdims=True) * (1.0 / D)
    spread = jnp.sum(center * center, axis=-1, keepdims=True) * (1.0 / D)
    return center * lax.rsqrt(spread + NORM_EPS)


def tail_kernel(slides, ctxs, emb_ref, slide_ref, pos_ref, len_ref, wqkv_hbm, wout_hbm, out_ref,
                wqkv_ref, wout_ref, send_ref, recv_ref, rows_ref, k_ref, v_ref, q_ref, att_ref,
                load_sem, a2a_send, a2a_recv, own_sem, ring_send, ring_recv):
    count = slides * ctxs
    tiles = emb_ref.shape[0]
    total = ctxs * SEQ_DEV
    slide = lax.axis_index("slide")
    ctx = lax.axis_index("ctx")
    me = slide * ctxs + ctx
    barrier = pltpu.get_barrier_semaphore()

    def greet(k, _):
        peer = lax.rem(me + k, count)
        pl.semaphore_signal(barrier, inc=1, device_id=(peer // ctxs, lax.rem(peer, ctxs)), device_id_type=MESH)
        return 0
    lax.fori_loop(1, count, greet, 0)
    load_qkv = pltpu.make_async_copy(wqkv_hbm, wqkv_ref, load_sem.at[0])
    load_out = pltpu.make_async_copy(wout_hbm, wout_ref, load_sem.at[1])
    load_qkv.start()
    load_out.start()

    pos = pos_ref[...].reshape(1, tiles).astype(jnp.float32)
    block = jnp.floor((pos + 0.5) * (1.0 / SEQ_DEV))
    owner = slide_ref[...].reshape(1, tiles).astype(jnp.float32) * ctxs + block
    code = pos - block * SEQ_DEV + 1.0
    line = lax.broadcasted_iota(jnp.int32, (count * CAP, tiles), 0)
    target = (line // CAP).astype(jnp.float32)
    member = jnp.where(owner == target, 1.0, 0.0)
    before = lax.broadcasted_iota(jnp.int32, (tiles, tiles), 0) < lax.broadcasted_iota(jnp.int32, (tiles, tiles), 1)
    rank = jnp.dot(member.astype(jnp.bfloat16), jnp.where(before, 1.0, 0.0).astype(jnp.bfloat16),
                   preferred_element_type=jnp.float32)
    chosen = jnp.where(rank == (line % CAP).astype(jnp.float32), member, 0.0)
    codes = jnp.broadcast_to(jnp.sum(chosen * code, axis=1, keepdims=True), (count * CAP, 128))
    moved = jnp.dot(chosen.astype(jnp.bfloat16), emb_ref[...], preferred_element_type=jnp.float32)
    send_ref[:, :, :D] = moved.reshape(count, CAP, D).astype(jnp.bfloat16)
    send_ref[:, :, D:] = codes.reshape(count, CAP, 128).astype(jnp.bfloat16)
    pl.semaphore_wait(barrier, count - 1)

    own = pltpu.make_async_copy(send_ref.at[me], recv_ref.at[me], own_sem)
    own.start()

    def send(k, _):
        peer = lax.rem(me + k, count)
        pltpu.make_async_remote_copy(
            src_ref=send_ref.at[peer], dst_ref=recv_ref.at[me], send_sem=a2a_send, recv_sem=a2a_recv,
            device_id=(peer // ctxs, lax.rem(peer, ctxs)), device_id_type=MESH).start()
        return 0
    lax.fori_loop(1, count, send, 0)
    own.wait()
    rest = pl.ds(0, count - 1)
    whole = pltpu.make_async_remote_copy(
        src_ref=send_ref.at[rest], dst_ref=recv_ref.at[rest], send_sem=a2a_send, recv_sem=a2a_recv,
        device_id=(slide, ctx), device_id_type=MESH)
    whole.wait_recv()

    arrived = recv_ref[...].reshape(count * CAP, CODED)
    got = arrived[:, D:].astype(jnp.float32)
    lane = lax.broadcasted_iota(jnp.int32, (count * CAP, 128), 1).astype(jnp.float32) + 1.0
    pick = jnp.concatenate([jnp.where(got == lane, 1.0, 0.0), jnp.where(got == lane + 128.0, 1.0, 0.0)], axis=1)
    mine = lax.dot_general(pick.astype(jnp.bfloat16), arrived[:, :D], (((0,), (0,)), ((), ())),
                           preferred_element_type=jnp.float32)
    rows_ref[ctx] = mine[:SEQ_DEV].astype(jnp.bfloat16)

    right = lax.rem(ctx + 1, ctxs)
    left = lax.rem(ctx + ctxs - 1, ctxs)
    far = lax.rem(ctx + 2, ctxs)
    first, second = pl.ds(0, HALF_SEQ), pl.ds(HALF_SEQ, HALF_SEQ)

    def hop(n, blk, half, to):
        return pltpu.make_async_remote_copy(
            src_ref=rows_ref.at[blk, half], dst_ref=rows_ref.at[blk, half],
            send_sem=ring_send.at[n], recv_sem=ring_recv.at[n], device_id=(slide, to), device_id_type=MESH)

    def keys_values(blk):
        ln = row_norm(rows_ref[blk].astype(jnp.float32)).astype(jnp.bfloat16)
        at = pl.ds(pl.multiple_of(blk * SEQ_DEV, 64), SEQ_DEV)
        k_ref[at, :] = jnp.dot(ln, wqkv_ref[:, D:2 * D], preferred_element_type=jnp.float32).astype(jnp.bfloat16)
        v_ref[at, :] = jnp.dot(ln, wqkv_ref[:, 2 * D:], preferred_element_type=jnp.float32).astype(jnp.bfloat16)
        return ln
    own_hops = [hop(0, ctx, first, right), hop(1, ctx, second, left), hop(2, ctx, second, right), hop(3, ctx, first, left)]
    for h in own_hops:
        h.start()
    load_qkv.wait()
    ln = keys_values(ctx)
    q = jnp.dot(ln, wqkv_ref[:, :D], preferred_element_type=jnp.float32)
    q_ref[...] = (q.astype(jnp.bfloat16).astype(jnp.float32) * HEAD_DIM ** (-0.5)).astype(jnp.bfloat16)
    own_hops[0].wait_recv()
    onward = hop(4, left, first, right)
    onward.start()
    own_hops[1].wait_recv()
    back = hop(5, right, second, left)
    back.start()
    own_hops[2].wait_recv()
    own_hops[3].wait_recv()

    def near(n, _):
        keys_values(lax.rem(ctx + 1 + 2 * n, ctxs))
        return 0
    lax.fori_loop(0, 2, near, 0)
    onward.wait_recv()
    back.wait_recv()
    keys_values(far)
    for h in own_hops + [onward, back]:
        h.wait_send()
    whole.wait_send()
    load_out.wait()

    length = len_ref[slide]
    key = lax.broadcasted_iota(jnp.int32, (1, total), 1)
    bias = jnp.where(key < length, 0.0, FAR_NEGATIVE)
    low = lax.broadcasted_iota(jnp.int32, (SEQ_DEV, 128), 1) < HEAD_DIM
    for pair in range(HEADS // 2):
        cols = slice(pair * 128, pair * 128 + 128)
        q2 = q_ref[:, cols]
        zero = jnp.zeros_like(q2)
        both = jnp.concatenate([jnp.where(low, q2, zero), jnp.where(low, zero, q2)], axis=0)
        s = lax.dot_general(both, k_ref[:, cols], (((1,), (1,)), ((), ())), preferred_element_type=jnp.float32) + bias
        w = jnp.exp(s - jnp.max(s, axis=-1, keepdims=True))
        denom = jnp.sum(w, axis=-1, keepdims=True)
        o = jnp.dot(w.astype(jnp.bfloat16), v_ref[:, cols], preferred_element_type=jnp.float32) / denom
        att_ref[:, cols] = jnp.where(low, o[:SEQ_DEV], o[SEQ_DEV:]).astype(jnp.bfloat16)
    out = jnp.dot(att_ref[...], wout_ref[...], preferred_element_type=jnp.float32)
    out = out + rows_ref[ctx].astype(jnp.float32)
    row = lax.broadcasted_iota(jnp.int32, (SEQ_DEV, 1), 0) + ctx * SEQ_DEV
    out_ref[...] = jnp.where(row < length, out, 0.0).astype(jnp.bfloat16)


def slide_layer(embeds, tile_slide, tile_pos, slide_len, wqkv, wout, slides, ctxs):
    count = slides * ctxs
    total = ctxs * SEQ_DEV
    vmem = pl.BlockSpec(memory_space=pltpu.VMEM)
    hbm = pl.BlockSpec(memory_space=pl.ANY)
    return pl.pallas_call(
        functools.partial(tail_kernel, slides, ctxs),
        out_shape=jax.ShapeDtypeStruct((SEQ_DEV, D), jnp.bfloat16),
        in_specs=[vmem, vmem, vmem, pl.BlockSpec(memory_space=pltpu.SMEM), hbm, hbm],
        out_specs=vmem,
        scratch_shapes=[
            pltpu.VMEM((D, 3 * D), jnp.bfloat16), pltpu.VMEM((D, D), jnp.bfloat16),
            pltpu.VMEM((count, CAP, CODED), jnp.bfloat16), pltpu.VMEM((count, CAP, CODED), jnp.bfloat16),
            pltpu.VMEM((ctxs, SEQ_DEV, D), jnp.bfloat16),
            pltpu.VMEM((total, D), jnp.bfloat16), pltpu.VMEM((total, D), jnp.bfloat16),
            pltpu.VMEM((SEQ_DEV, D), jnp.bfloat16), pltpu.VMEM((SEQ_DEV, D), jnp.bfloat16),
            pltpu.SemaphoreType.DMA((2,)),
            pltpu.SemaphoreType.DMA, pltpu.SemaphoreType.DMA, pltpu.SemaphoreType.DMA,
            pltpu.SemaphoreType.DMA((6,)), pltpu.SemaphoreType.DMA((6,)),
        ],
        compiler_params=pltpu.CompilerParams(collective_id=0, has_side_effects=True, vmem_limit_bytes=48 << 20),
        name="slide_layer",
    )(embeds, tile_slide, tile_pos, slide_len, wqkv, wout)


def shards(feature_maps, down_weight, conv_taps, mlp_in, mlp_out, layer_scale, qkv_weight, out_weight,
           tile_slide, tile_pos, slide_len):
    embeds = encode_tiles(feature_maps, down_weight, conv_taps, mlp_in, mlp_out, layer_scale)
    return slide_layer(embeds, tile_slide, tile_pos, slide_len, qkv_weight[0], out_weight[0],
                       lax.axis_size("slide"), lax.axis_size("ctx"))


def solution(mesh):
    whole = P(("slide", "ctx"))
    return jax.shard_map(
        shards,
        mesh=mesh,
        in_specs=(whole, P(), P(), P(), P(), P(), P(), P(), whole, whole, P()),
        out_specs=whole,
        check_vma=False,
    )
```

time: 104 us -> 84.3 us (0.81)
  Pallas kernels: 92.7 us -> 82.5 us
  local copies, waits for them, and re-layouts: 7.11 us -> 1.53 us
  matrix products: 1.82 us -> 0 us
  other arithmetic: 1.58 us -> 0 us
    pallas_call x3 -> x2, Pallas kernels: 92.7 us -> 82.5 us  [the longest x1 46.5 us: encode_tiles(): pl.pallas_call(functools.partial(encode_kernel, groups), out_shape=jax.Sh...]
    reshape x2 -> x0, local copies, waits for them, and re-layouts: 3.24 us -> none  [the longest x1 1.98 us: shards(): outgoing.reshape(slides * ctxs, CAP, CODED)]
    dot_general x1 -> x0, matrix products: 1.82 us -> none  [shards(): jnp.dot(placing.astype(jnp.bfloat16), coded, preferred_element_type=jnp.f...]
    dynamic_slice x1 -> x0, local copies, waits for them, and re-layouts: 1.26 us -> none  [shards(): slide_len[lax.axis_index('slide')]]
    unnamed x6 -> x13, local copies, waits for them, and re-layouts: 2.54 us -> 1.53 us
where the time goes in v3:
time: 84.3 us; the launch traced here: 84.1 us
  Pallas kernels  82.5 us (98%)
  local copies, waits for them, and re-layouts  1.53 us (2%)
    pallas_call x1, Pallas kernels, encode_tiles(): pl.pallas_call(functools.partial(encode_kernel, groups), out_shape=jax.Sh...  46.5 us
    pallas_call x1, Pallas kernels, slide_layer(): pl.pallas_call(functools.partial(tail_kernel, slides, ctxs), out_shape=ja...  36.1 us

profile of v3, /device:TPU:1, one launch (start us, length us, event | category | flops | bytes accessed | tf_op | source)
XLA Modules:
  0.0 84.1 jit_solution(3742227107094126826)
XLA Ops:
  0.0 0.0 copy-start
  0.0 0.0 copy-start.1
  0.0 0.0 copy-start.3
  0.0 0.0 copy-start.4
  0.0 0.0 copy-start.5
  0.0 46.5 %encode.1.emb_ref = bf16[32,768]{1,0:T(8,128)(2,1)} custom-call(bf16[32,16,16,384]{3,2,1,0:T(8,128)(2,1)} %x_hbm.1, bf16[1536,768]{1,0:T(8,128)(2,1)} %down_hbm.1, bf16[49,768]{1,0:T(8,128)(2,1)} %taps_ref.1, bf16[768,3072]{1,0:T(8,128)(2,1)} %w1_hbm.1, bf16[3072,768]{1,0:T(8,128)(2,1)} %w2_hbm.1, f32[768]{0:T(1024)} %ls_ref.1), custom_call_target="tpu_custom_call" | custom-call | tf_op jit(solution)/shard_map/encode/pallas_call | solution.py:194
  46.5 0.0 copy-done
  46.5 0.0 copy-done.1
  46.5 0.0 copy-done.3
  46.5 0.0 copy-done.4
  46.5 0.0 copy-done.5
  46.5 0.0 copy-start.2
  46.6 0.8 copy-done.2
  47.3 36.1 %slide_layer.1 = bf16[192,768]{1,0:T(8,128)(2,1)S(1)} custom-call(bf16[32,768]{1,0:T(8,128)(2,1)S(1)} %copy-done.2, s32[32]{0:T(128)S(1)} %copy-done.3, s32[32]{0:T(128)S(1)} %copy-done.4, s32[32]{0:T(128)S(1)} %copy-done.5, bf16[768,2304]{1,0:T(8,128)(2,1)S(1)} %bitcast.2, bf16[768,768]{1,0:T(8,128)(2,1)S(1)} %bitcast.3), custom_call_target="tpu_custom_call" | custom-call | tf_op jit(solution)/shard_map/slide_layer/pallas_call | solution.py:371
  83.4 0.7 copy.13
Async XLA Ops:
  0.0 46.5 %copy-start = (bf16[1,768,2304]{2,1,0:T(8,128)(2,1)S(1)}, bf16[1,768,2304]{2,1,0:T(8,128)(2,1)}, u32[]{:S(2)}) copy-start(bf16[1,768,2304]{2,1,0:T(8,128)(2,1)} %param.17) | copy-start | bytes 10616836
  0.0 46.5 %copy-start.1 = (bf16[1,768,768]{2,1,0:T(8,128)(2,1)S(1)}, bf16[1,768,768]{2,1,0:T(8,128)(2,1)}, u32[]{:S(2)}) copy-start(bf16[1,768,768]{2,1,0:T(8,128)(2,1)} %param.18) | copy-start | bytes 3538948
  0.0 46.5 %copy-start.3 = (s32[32]{0:T(128)S(1)}, s32[32]{0:T(128)}, u32[]{:S(2)}) copy-start(s32[32]{0:T(128)} %slide_ref.1) | copy-start | bytes 388
  0.0 46.5 %copy-start.4 = (s32[32]{0:T(128)S(1)}, s32[32]{0:T(128)}, u32[]{:S(2)}) copy-start(s32[32]{0:T(128)} %pos_ref.1) | copy-start | bytes 388
  0.0 46.5 %copy-start.5 = (s32[32]{0:T(128)S(1)}, s32[32]{0:T(128)}, u32[]{:S(2)}) copy-start(s32[32]{0:T(128)} %len_ref.1) | copy-start | bytes 388
  46.5 0.8 copy-start.2

commit v4 on v3

--- a/solution.py
+++ b/solution.py
@@ -5,6 +5,7 @@
 from jax import lax
 from jax.experimental import pallas as pl
 from jax.experimental.pallas import tpu as pltpu
+from jax.sharding import PartitionSpec as P
 
 NORM_EPS = 1e-06
 GROUP = 8
@@ -17,6 +18,7 @@
 HC = 512
 PITCH = 257
 INV_SQRT2 = 0.7071067811865476
+BSPLIT = 2
 
 
 def split_bf16(values):
@@ -24,28 +26,15 @@
     return high, (values - high.astype(jnp.float32)).astype(jnp.bfloat16)
 
 
-def lane_total(values, ones):
-    return jnp.dot(jnp.concatenate(split_bf16(values), axis=-1), ones, preferred_element_type=jnp.float32)
-
-
-def norm_maps(x_ref, s_ref, g):
-    ones = jnp.full((256, 128), 1.0, jnp.bfloat16)
-    inv_n = 1.0 / C_IN
-
-    def one_tile(t, _):
-        def parts():
-            x = x_ref[g * GROUP + t].reshape(256, C_IN)
-            return [x[:, l * 128:(l + 1) * 128].astype(jnp.float32) for l in range(3)]
-        xs = parts()
-        mean = lane_total(xs[0] + xs[1] + xs[2], ones) * inv_n
-        cs = [x - mean for x in xs]
-        var = lane_total(cs[0] * cs[0] + cs[1] * cs[1] + cs[2] * cs[2], ones) * inv_n
-        inv = lax.rsqrt(var + NORM_EPS)
-        for l in range(3):
-            s_ref[l, pl.ds(t * PITCH, 256), :] = cs[l] * inv
-        return 0
-
-    lax.fori_loop(0, GROUP, one_tile, 0, unroll=2)
+def norm_rows(n, x_ref, s_ref, g):
+    t = n // 4
+    y = (n % 4) * 4
+    x = x_ref[g * GROUP + t, pl.ds(y, 4)].reshape(64, C_IN).astype(jnp.float32)
+    c = x - jnp.sum(x, axis=-1, keepdims=True) * (1.0 / C_IN)
+    v = jnp.sum(c * c, axis=-1, keepdims=True) * (1.0 / C_IN)
+    o = c * lax.rsqrt(v + NORM_EPS)
+    for l in range(3):
+        s_ref[l, pl.ds(t * PITCH + y * 16, 64), :] = o[:, l * 128:(l + 1) * 128]
 
 
 def make_patches(s_ref, l_ref):
@@ -65,12 +54,13 @@
     lax.fori_loop(0, HALF * HALF // 2, patch_rows, 0, unroll=2)
 
 
-def reduce_chunk(n, l_ref, down_ref, r_ref):
-    cols = pl.ds(pl.multiple_of(n * 256, 256), 256)
-    red = jnp.dot(l_ref[...], down_ref[:, cols], preferred_element_type=jnp.float32)
+def reduce_rows(m, l_ref, down_ref, r_ref):
+    rows = 64 * GROUP // BSPLIT
+    lhs = l_ref[pl.ds(pl.multiple_of(m * rows, rows), rows), :]
+    red = jnp.dot(lhs, down_ref[...], preferred_element_type=jnp.float32)
     red = red.astype(jnp.bfloat16).astype(jnp.float32)
-    for h in range(2):
-        r_ref[n * 2 + h] = red[:, h * 128:(h + 1) * 128].reshape(64, GROUP, 128)
+    for h in range(LB):
+        r_ref[h, pl.ds(m * (rows // GROUP), rows // GROUP)] = red[:, h * 128:(h + 1) * 128].reshape(rows // GROUP, GROUP, 128)
 
 
 def conv_lane(l, r_ref, tap_ref, sp_ref, pr_ref, g):
@@ -105,28 +95,27 @@
         cs = [r - mean for r in rows]
         sq = [c * c for c in cs]
         sq = ((sq[0] + sq[1]) + (sq[2] + sq[3])) + (sq[4] + sq[5])
-        inv = lax.rsqrt(jnp.sum(sq, axis=-1, keepdims=True) * (1.0 / D) + NORM_EPS)
+        inv = lax.rsqrt(jnp.sum(sq, axis=-1, keepdims=True) * (1.0 / D) + NORM_EPS) * INV_SQRT2
         for l in range(LB):
             sn_ref[pl.ds(pl.multiple_of(n * 64, 64), 64), l * 128:(l + 1) * 128] = (cs[l] * inv).astype(jnp.bfloat16)
         return 0
-    lax.fori_loop(0, 8, some_rows, 0, unroll=4)
+    lax.fori_loop(0, 8, some_rows, 0, unroll=8)
 
 
 def hidden_chunk(c, sn_ref, w1_ref, ph_ref, g):
-    cols = pl.ds(pl.multiple_of(c * HC, HC), HC)
-    h = jnp.dot(sn_ref[...], w1_ref[:, cols], preferred_element_type=jnp.float32)
-    h = h + h * lax.erf(h * INV_SQRT2)
-    ph_ref[g * GROUP:(g + 1) * GROUP, cols] = jnp.sum(h.reshape(64, GROUP, HC), axis=0)
-
-
-def encode_kernel(groups, x_hbm, down_hbm, taps_ref, w1_hbm, w2_hbm, ls_ref, out_ref,
+    h = jnp.dot(sn_ref[...], w1_ref[c], preferred_element_type=jnp.float32)
+    h = h + h * lax.erf(h)
+    ph_ref[c, g * GROUP:(g + 1) * GROUP, :] = jnp.sum(h.reshape(64, GROUP, HC), axis=0)
+
+
+def encode(groups, more_loads, x_hbm, down_hbm, taps_ref, w1_hbm, w2_hbm, ls_ref, emb_ref,
                   x_ref, down_ref, w1_ref, w2_ref, s_ref, l0_ref, l1_ref, r0_ref, r1_ref, sp_ref, sn_ref, tap_ref, ph_ref, pr_ref, sems):
     l_bufs, r_bufs = (l0_ref, l1_ref), (r0_ref, r1_ref)
     x_copy = [pltpu.make_async_copy(x_hbm.at[pl.ds(g * GROUP, GROUP)], x_ref.at[pl.ds(g * GROUP, GROUP)], sems.at[g])
               for g in range(groups)]
     down_copy = pltpu.make_async_copy(down_hbm, down_ref, sems.at[groups])
-    w1_copy = pltpu.make_async_copy(w1_hbm, w1_ref, sems.at[groups + 1])
-    w2_copy = pltpu.make_async_copy(w2_hbm, w2_ref, sems.at[groups + 2])
+    w1_copy = [pltpu.make_async_copy(w1_hbm.at[:, pl.ds(c * HC, HC)], w1_ref.at[c], sems.at[groups + 2 + c]) for c in range(LB)]
+    w2_copy = pltpu.make_async_copy(w2_hbm, w2_ref, sems.at[groups + 1])
     x_copy[0].start()
     down_copy.start()
     t = taps_ref[...].astype(jnp.float32)
@@ -135,90 +124,64 @@
             tap_ref[l, k] = jnp.broadcast_to(t[k:k + 1, l * 128:(l + 1) * 128], (8, 128))
     x_copy[0].wait()
     x_copy[1].start()
-    w1_copy.start()
-    norm_maps(x_ref, s_ref, 0)
+    for copy in w1_copy:
+        copy.start()
+    def only_norm(n, _):
+        norm_rows(n, x_ref, s_ref, 0)
+        return 0
+    lax.fori_loop(0, GROUP * 4, only_norm, 0, unroll=8)
     make_patches(s_ref, l0_ref)
     for g in range(2, groups):
         x_copy[g].start()
     w2_copy.start()
+    for copy in more_loads:
+        copy.start()
     down_copy.wait()
 
-    def first(n, _):
-        reduce_chunk(n, l0_ref, down_ref, r0_ref)
-        return 0
-    lax.fori_loop(0, 3, first, 0)
-    x_copy[1].wait()
-    norm_maps(x_ref, s_ref, 1)
-    make_patches(s_ref, l1_ref)
+    def norm_and_reduce(g_norm, g_red):
+        per = GROUP * 4 // BSPLIT
+
+        def step(n, _):
+            if g_norm < groups:
+                for k in range(per):
+                    norm_rows(n * per + k, x_ref, s_ref, g_norm)
+            if g_red < groups:
+                reduce_rows(n, l_bufs[g_red % 2], down_ref, r_bufs[g_red % 2])
+            return 0
+        if g_norm < groups:
+            x_copy[g_norm].wait()
+        lax.fori_loop(0, BSPLIT, step, 0)
+        if g_norm < groups:
+            make_patches(s_ref, l_bufs[g_norm % 2])
+    norm_and_reduce(1, 0)
 
     for g in range(groups + 1):
         if g == 1:
-            w1_copy.wait()
+            for copy in w1_copy:
+                copy.wait()
 
         def step(n, _):
+            if g < groups:
+                conv_lane(n, r_bufs[g % 2], tap_ref, sp_ref, pr_ref, g)
             if g >= 1:
-                hidden_chunk(2 * n, sn_ref, w1_ref, ph_ref, g - 1)
-            if g < groups:
-                conv_lane(2 * n, r_bufs[g % 2], tap_ref, sp_ref, pr_ref, g)
-            if g >= 1:
-                hidden_chunk(2 * n + 1, sn_ref, w1_ref, ph_ref, g - 1)
-            if g < groups:
-                conv_lane(2 * n + 1, r_bufs[g % 2], tap_ref, sp_ref, pr_ref, g)
-            if g + 1 < groups:
-                reduce_chunk(n, l_bufs[(g + 1) % 2], down_ref, r_bufs[(g + 1) % 2])
+                hidden_chunk(n, sn_ref, w1_ref, ph_ref, g - 1)
             return 0
-        lax.fori_loop(0, 3, step, 0)
+        lax.fori_loop(0, LB, step, 0, unroll=3 if g == groups else 1)
         if g < groups:
             norm_spatial(sp_ref, sn_ref)
-        if g + 2 < groups:
-            x_copy[g + 2].wait()
-            norm_maps(x_ref, s_ref, g + 2)
-            make_patches(s_ref, l_bufs[g % 2])
+        if g + 1 < groups:
+            norm_and_reduce(g + 2, g + 1)
 
     w2_copy.wait()
-    br = jnp.dot(jnp.concatenate(split_bf16(ph_ref[...]), axis=0), w2_ref[...], preferred_element_type=jnp.float32)
+    br = jnp.dot(jnp.concatenate(split_bf16(jnp.concatenate([ph_ref[c] for c in range(LB)], axis=-1)), axis=0), w2_ref[...], preferred_element_type=jnp.float32)
     nt = groups * GROUP
     br = br[:nt] + br[nt:]
     pr = jnp.concatenate([pr_ref[l] for l in range(LB)], axis=-1)
-    pooled = (pr + ls_ref[...].reshape(1, D) * (0.5 * br)) * (1.0 / (HALF * HALF))
+    pooled = (pr + ls_ref[...].reshape(1, D) * (INV_SQRT2 * br)) * (1.0 / (HALF * HALF))
     c = pooled - jnp.mean(pooled, axis=-1, keepdims=True)
     v = jnp.mean(c * c, axis=-1, keepdims=True)
-    out_ref[...] = (c * lax.rsqrt(v + NORM_EPS)).astype(jnp.bfloat16)
-
-
-def encode_tiles(x, down, taps, w1, w2, ls):
-    nt = x.shape[0]
-    groups = nt // GROUP
-    hbm = pl.BlockSpec(memory_space=pl.ANY)
-    vmem = pl.BlockSpec(memory_space=pltpu.VMEM)
-    return pl.pallas_call(
-        functools.partial(encode_kernel, groups),
-        out_shape=jax.ShapeDtypeStruct((nt, D), jnp.bfloat16),
-        in_specs=[hbm, hbm, vmem, hbm, hbm, vmem],
-        out_specs=vmem,
-        scratch_shapes=[
-            pltpu.VMEM((nt, 16, 16, C_IN), jnp.bfloat16),
-            pltpu.VMEM((4 * C_IN, D), jnp.bfloat16),
-            pltpu.VMEM((D, MLP), jnp.bfloat16),
-            pltpu.VMEM((MLP, D), jnp.bfloat16),
-            pltpu.VMEM((3, GROUP * PITCH, 128), jnp.float32),
-            pltpu.VMEM((64 * GROUP, 4 * C_IN), jnp.bfloat16),
-            pltpu.VMEM((64 * GROUP, 4 * C_IN), jnp.bfloat16),
-            pltpu.VMEM((LB, 64, GROUP, 128), jnp.float32),
-            pltpu.VMEM((LB, 64, GROUP, 128), jnp.float32),
-            pltpu.VMEM((LB, 64, GROUP, 128), jnp.float32),
-            pltpu.VMEM((64 * GROUP, D), jnp.bfloat16),
-            pltpu.VMEM((LB, KS * KS, 8, 128), jnp.float32),
-            pltpu.VMEM((nt, MLP), jnp.float32),
-            pltpu.VMEM((LB, nt, 128), jnp.float32),
-            pltpu.SemaphoreType.DMA((groups + 3,)),
-        ],
-        compiler_params=pltpu.CompilerParams(vmem_limit_bytes=56 << 20),
-        name="encode",
-    )(x, down, taps, w1, w2, ls)
-
-
-from jax.sharding import PartitionSpec as P
+    emb_ref[...] = (c * lax.rsqrt(v + NORM_EPS)).astype(jnp.bfloat16)
+
 
 HEADS = 12
 HEAD_DIM = 64
@@ -236,27 +199,28 @@
     return center * lax.rsqrt(spread + NORM_EPS)
 
 
-def tail_kernel(slides, ctxs, emb_ref, slide_ref, pos_ref, len_ref, wqkv_hbm, wout_hbm, out_ref,
+def greet(slides, ctxs):
+    count = slides * ctxs
+    me = lax.axis_index("slide") * ctxs + lax.axis_index("ctx")
+    barrier = pltpu.get_barrier_semaphore()
+
+    def one(k, _):
+        peer = lax.rem(me + k, count)
+        pl.semaphore_signal(barrier, inc=1, device_id=(peer // ctxs, lax.rem(peer, ctxs)), device_id_type=MESH)
+        return 0
+    lax.fori_loop(1, count, one, 0)
+
+
+def slide_layer(slides, ctxs, loads, emb_ref, slide_ref, pos_ref, len_ref, out_ref,
                 wqkv_ref, wout_ref, send_ref, recv_ref, rows_ref, k_ref, v_ref, q_ref, att_ref,
-                load_sem, a2a_send, a2a_recv, own_sem, ring_send, ring_recv):
+                a2a_send, a2a_recv, own_sem, ring_send, ring_recv):
+    load_qkv, load_out = loads
     count = slides * ctxs
     tiles = emb_ref.shape[0]
     total = ctxs * SEQ_DEV
     slide = lax.axis_index("slide")
     ctx = lax.axis_index("ctx")
     me = slide * ctxs + ctx
-    barrier = pltpu.get_barrier_semaphore()
-
-    def greet(k, _):
-        peer = lax.rem(me + k, count)
-        pl.semaphore_signal(barrier, inc=1, device_id=(peer // ctxs, lax.rem(peer, ctxs)), device_id_type=MESH)
-        return 0
-    lax.fori_loop(1, count, greet, 0)
-    load_qkv = pltpu.make_async_copy(wqkv_hbm, wqkv_ref, load_sem.at[0])
-    load_out = pltpu.make_async_copy(wout_hbm, wout_ref, load_sem.at[1])
-    load_qkv.start()
-    load_out.start()
-
     pos = pos_ref[...].reshape(1, tiles).astype(jnp.float32)
     block = jnp.floor((pos + 0.5) * (1.0 / SEQ_DEV))
     owner = slide_ref[...].reshape(1, tiles).astype(jnp.float32) * ctxs + block
@@ -272,7 +236,7 @@
     moved = jnp.dot(chosen.astype(jnp.bfloat16), emb_ref[...], preferred_element_type=jnp.float32)
     send_ref[:, :, :D] = moved.reshape(count, CAP, D).astype(jnp.bfloat16)
     send_ref[:, :, D:] = codes.reshape(count, CAP, 128).astype(jnp.bfloat16)
-    pl.semaphore_wait(barrier, count - 1)
+    pl.semaphore_wait(pltpu.get_barrier_semaphore(), count - 1)
 
     own = pltpu.make_async_copy(send_ref.at[me], recv_ref.at[me], own_sem)
     own.start()
@@ -363,36 +327,58 @@
     out_ref[...] = jnp.where(row < length, out, 0.0).astype(jnp.bfloat16)
 
 
-def slide_layer(embeds, tile_slide, tile_pos, slide_len, wqkv, wout, slides, ctxs):
+def whole_kernel(groups, slides, ctxs, x_hbm, down_hbm, taps_ref, w1_hbm, w2_hbm, ls_ref, wqkv_hbm, wout_hbm,
+                 slide_ref, pos_ref, len_ref, out_ref, emb_ref, load_sem, wqkv_ref, wout_ref, send_ref, recv_ref, rows_ref,
+                 k_ref, v_ref, q_ref, att_ref, a2a_send, a2a_recv, own_sem, ring_send, ring_recv, *encoder_refs):
+    greet(slides, ctxs)
+    loads = (pltpu.make_async_copy(wqkv_hbm, wqkv_ref, load_sem.at[0]), pltpu.make_async_copy(wout_hbm, wout_ref, load_sem.at[1]))
+    encode(groups, loads, x_hbm, down_hbm, taps_ref, w1_hbm, w2_hbm, ls_ref, emb_ref, *encoder_refs)
+    slide_layer(slides, ctxs, loads, emb_ref, slide_ref, pos_ref, len_ref, out_ref,
+                wqkv_ref, wout_ref, send_ref, recv_ref, rows_ref, k_ref, v_ref, q_ref, att_ref,
+                a2a_send, a2a_recv, own_sem, ring_send, ring_recv)
+
+
+def shards(x, down, taps, w1, w2, ls, qkv_weight, out_weight, tile_slide, tile_pos, slide_len):
+    slides, ctxs = lax.axis_size("slide"), lax.axis_size("ctx")
+    nt = x.shape[0]
+    groups = nt // GROUP
     count = slides * ctxs
     total = ctxs * SEQ_DEV
+    hbm = pl.BlockSpec(memory_space=pl.ANY)
     vmem = pl.BlockSpec(memory_space=pltpu.VMEM)
-    hbm = pl.BlockSpec(memory_space=pl.ANY)
     return pl.pallas_call(
-        functools.partial(tail_kernel, slides, ctxs),
+        functools.partial(whole_kernel, groups, slides, ctxs),
         out_shape=jax.ShapeDtypeStruct((SEQ_DEV, D), jnp.bfloat16),
-        in_specs=[vmem, vmem, vmem, pl.BlockSpec(memory_space=pltpu.SMEM), hbm, hbm],
+        in_specs=[hbm, hbm, vmem, hbm, hbm, vmem, hbm, hbm, vmem, vmem, pl.BlockSpec(memory_space=pltpu.SMEM)],
         out_specs=vmem,
         scratch_shapes=[
+            pltpu.VMEM((nt, D), jnp.bfloat16), pltpu.SemaphoreType.DMA((2,)),
             pltpu.VMEM((D, 3 * D), jnp.bfloat16), pltpu.VMEM((D, D), jnp.bfloat16),
             pltpu.VMEM((count, CAP, CODED), jnp.bfloat16), pltpu.VMEM((count, CAP, CODED), jnp.bfloat16),
             pltpu.VMEM((ctxs, SEQ_DEV, D), jnp.bfloat16),
             pltpu.VMEM((total, D), jnp.bfloat16), pltpu.VMEM((total, D), jnp.bfloat16),
             pltpu.VMEM((SEQ_DEV, D), jnp.bfloat16), pltpu.VMEM((SEQ_DEV, D), jnp.bfloat16),
-            pltpu.SemaphoreType.DMA((2,)),
             pltpu.SemaphoreType.DMA, pltpu.SemaphoreType.DMA, pltpu.SemaphoreType.DMA,
             pltpu.SemaphoreType.DMA((6,)), pltpu.SemaphoreType.DMA((6,)),
+            pltpu.VMEM((nt, 16, 16, C_IN), jnp.bfloat16),
+            pltpu.VMEM((4 * C_IN, D), jnp.bfloat16),
+            pltpu.VMEM((LB, D, HC), jnp.bfloat16),
+            pltpu.VMEM((MLP, D), jnp.bfloat16),
+            pltpu.VMEM((3, GROUP * PITCH, 128), jnp.float32),
+            pltpu.VMEM((64 * GROUP, 4 * C_IN), jnp.bfloat16),
+            pltpu.VMEM((64 * GROUP, 4 * C_IN), jnp.bfloat16),
+            pltpu.VMEM((LB, 64, GROUP, 128), jnp.float32),
+            pltpu.VMEM((LB, 64, GROUP, 128), jnp.float32),
+            pltpu.VMEM((LB, 64, GROUP, 128), jnp.float32),
+            pltpu.VMEM((64 * GROUP, D), jnp.bfloat16),
+            pltpu.VMEM((LB, KS * KS, 8, 128), jnp.float32),
+            pltpu.VMEM((LB, nt, HC), jnp.float32),
+            pltpu.VMEM((LB, nt, 128), jnp.float32),
+            pltpu.SemaphoreType.DMA((groups + 2 + LB,)),
         ],
-        compiler_params=pltpu.CompilerParams(collective_id=0, has_side_effects=True, vmem_limit_bytes=48 << 20),
-        name="slide_layer",
-    )(embeds, tile_slide, tile_pos, slide_len, wqkv, wout)
-
-
-def shards(feature_maps, down_weight, conv_taps, mlp_in, mlp_out, layer_scale, qkv_weight, out_weight,
-           tile_slide, tile_pos, slide_len):
-    embeds = encode_tiles(feature_maps, down_weight, conv_taps, mlp_in, mlp_out, layer_scale)
-    return slide_layer(embeds, tile_slide, tile_pos, slide_len, qkv_weight[0], out_weight[0],
-                       lax.axis_size("slide"), lax.axis_size("ctx"))
+        compiler_params=pltpu.CompilerParams(collective_id=0, has_side_effects=True, vmem_limit_bytes=60 << 20),
+        name="whole",
+    )(x, down, taps, w1, w2, ls, qkv_weight[0], out_weight[0], tile_slide, tile_pos, slide_len)
 
 
 def solution(mesh):

time: 84.3 us -> 70.5 us (0.84)
  Pallas kernels: 82.5 us -> 68.6 us
    pallas_call x2 -> x1, Pallas kernels: 82.5 us -> 68.6 us  [shards(): pl.pallas_call(functools.partial(whole_kernel, groups, slides, ctxs), out...]
    unnamed x13 -> x1, local copies, waits for them, and re-layouts: 1.53 us -> 1.69 us
where the time goes in v4:
time: 70.5 us; the launch traced here: 70.3 us
  Pallas kernels  68.6 us (97%)
  local copies, waits for them, and re-layouts  1.69 us (2%)
    pallas_call x1, Pallas kernels, shards(): pl.pallas_call(functools.partial(whole_kernel, groups, slides, ctxs), out...  68.6 us
    unnamed x1, local copies, waits for them, and re-layouts  1.69 us

profile of v4, /device:TPU:1, one launch (start us, length us, event | category | flops | bytes accessed | tf_op | source)
XLA Modules:
  0.0 70.3 jit_solution(7848996371147594330)
XLA Ops:
  0.0 68.6 %whole.1 = bf16[192,768]{1,0:T(8,128)(2,1)} custom-call(bf16[32,16,16,384]{3,2,1,0:T(8,128)(2,1)} %x_hbm.1, bf16[1536,768]{1,0:T(8,128)(2,1)} %down_hbm.1, bf16[49,768]{1,0:T(8,128)(2,1)} %taps_ref.1, bf16[768,3072]{1,0:T(8,128)(2,1)} %w1_hbm.1, bf16[3072,768]{1,0:T(8,128)(2,1)} %w2_hbm.1, f32[768]{0:T(1024)} %ls_ref.1, bf16[768,2304]{1,0:T(8,128)(2,1)} %bitcast.2, ...), custom_call_target="tpu_custom_call" | custom-call | tf_op jit(solution)/shard_map/whole/pallas_call | solution.py:349
  68.6 1.7 %copy.13 = bf16[192,768]{1,0:T(8,128)(2,1)} copy(bf16[192,768]{1,0:T(8,128)(2,1)} %whole.1) | data formatting | bytes 589824

commit v5 on v4

--- a/solution.py
+++ b/solution.py
@@ -63,28 +63,89 @@
         r_ref[h, pl.ds(m * (rows // GROUP), rows // GROUP)] = red[:, h * 128:(h + 1) * 128].reshape(rows // GROUP, GROUP, 128)
 
 
-def conv_lane(l, r_ref, tap_ref, sp_ref, pr_ref, g):
+def tap_axis(part):
+    odd = {k: (2 * k + 3,) for k in (-1, 0, 1)}
+    even = {k: (2 * k + 2,) for k in (-1, 0, 1, 2)}
+    if part == 0:
+        return odd
+    if part == 1:
+        return even
+    return {k: even[k] + odd.get(k, ()) for k in even}
+
+
+TAP_SUMS = []
+TAP_AT = {}
+for _p in range(3):
+    for _q in range(3):
+        for _k, _ra in tap_axis(_p).items():
+            for _l, _cb in tap_axis(_q).items():
+                TAP_AT[(_p, _q, _k, _l)] = len(TAP_SUMS)
+                TAP_SUMS.append([a * KS + b for a in _ra for b in _cb])
+
+
+def fill_taps(taps_ref, tap_ref):
+    t = taps_ref[...].astype(jnp.float32)
+    for n, sums in enumerate(TAP_SUMS):
+        row = t[sums[0]:sums[0] + 1]
+        for k in sums[1:]:
+            row = row + t[k:k + 1]
+        for l in range(LB):
+            tap_ref[l, n] = jnp.broadcast_to(row[:, l * 128:(l + 1) * 128], (8, 128))
+
+
+def conv_lane(l, r_ref, tap_ref, sp_ref, pr_ref, x_tmp, y_tmp, g):
+    spots = range(4)
     psum = None
     for i in range(HALF):
-        acc = [None] * HALF
-        for a in range(KS):
-            ii = i + a - 3
-            if not 0 <= ii < HALF:
-                continue
-            xs = [r_ref[l, ii * HALF + j] for j in range(HALF)]
-            for b in range(KS):
-                w = tap_ref[l, a * KS + b]
-                for j in range(HALF):
-                    jj = j + b - 3
-                    if 0 <= jj < HALF:
-                        term = xs[jj] * w
-                        acc[j] = term if acc[j] is None else acc[j] + term
-            if ii == i:
-                row = ((xs[0] + xs[1]) + (xs[2] + xs[3])) + ((xs[4] + xs[5]) + (xs[6] + xs[7]))
-                psum = row if psum is None else psum + row
+        xs = [r_ref[l, i * HALF + j] for j in range(HALF)]
+        for j in spots:
+            x_tmp[i, 2, j] = xs[2 * j] + xs[2 * j + 1]
+    for i in spots:
+        row = None
+        for q in range(3):
+            for j in spots:
+                top = r_ref[l, 2 * i * HALF + 2 * j + q] if q < 2 else x_tmp[2 * i, 2, j]
+                low = r_ref[l, (2 * i + 1) * HALF + 2 * j + q] if q < 2 else x_tmp[2 * i + 1, 2, j]
+                both = top + low
+                x_tmp[8 + i, q, j] = both
+                if q == 2:
+                    row = both if row is None else row + both
+        psum = row if psum is None else psum + row
+    pr_ref[l, g * GROUP:(g + 1) * GROUP, :] = psum
+
+    def load(p, q, i, j):
+        if p == 2:
+            return x_tmp[8 + i, q, j]
+        if q == 2:
+            return x_tmp[2 * i + p, 2, j]
+        return r_ref[l, (2 * i + p) * HALF + 2 * j + q]
+
+    outs = [range(4), range(-1, 4), range(4)]
+    base = [0, 5, 9]
+    for p in range(3):
+        for i in outs[p]:
+            part = []
+            for q in range(3):
+                acc = {}
+                for k in tap_axis(p):
+                    if not 0 <= i + k < 4:
+                        continue
+                    xs = [load(p, q, i + k, j) for j in spots]
+                    for m in tap_axis(q):
+                        w = tap_ref[l, TAP_AT[(p, q, k, m)]]
+                        for j in outs[q]:
+                            if 0 <= j + m < 4:
+                                term = xs[j + m] * w
+                                acc[j] = acc[j] + term if j in acc else term
+                part.append(acc)
+            for j in spots:
+                y_tmp[base[p] + i, 2 * j] = part[0][j] + part[1][j - 1]
+                y_tmp[base[p] + i, 2 * j + 1] = part[2][j] - part[0][j] - part[1][j]
+    for i in spots:
         for j in range(HALF):
-            sp_ref[l, i * HALF + j] = acc[j]
-    pr_ref[l, g * GROUP:(g + 1) * GROUP, :] = psum
+            a, b, before, c = y_tmp[i, j], y_tmp[5 + i, j], y_tmp[4 + i, j], y_tmp[9 + i, j]
+            sp_ref[l, 2 * i * HALF + j] = a + before
+            sp_ref[l, (2 * i + 1) * HALF + j] = c - a - b
 
 
 def norm_spatial(sp_ref, sn_ref):
@@ -109,7 +170,7 @@
 
 
 def encode(groups, more_loads, x_hbm, down_hbm, taps_ref, w1_hbm, w2_hbm, ls_ref, emb_ref,
-                  x_ref, down_ref, w1_ref, w2_ref, s_ref, l0_ref, l1_ref, r0_ref, r1_ref, sp_ref, sn_ref, tap_ref, ph_ref, pr_ref, sems):
+                  x_ref, down_ref, w1_ref, w2_ref, s_ref, l0_ref, l1_ref, r0_ref, r1_ref, sp_ref, sn_ref, tap_ref, x_tmp, y_tmp, ph_ref, pr_ref, sems):
     l_bufs, r_bufs = (l0_ref, l1_ref), (r0_ref, r1_ref)
     x_copy = [pltpu.make_async_copy(x_hbm.at[pl.ds(g * GROUP, GROUP)], x_ref.at[pl.ds(g * GROUP, GROUP)], sems.at[g])
               for g in range(groups)]
@@ -118,10 +179,7 @@
     w2_copy = pltpu.make_async_copy(w2_hbm, w2_ref, sems.at[groups + 1])
     x_copy[0].start()
     down_copy.start()
-    t = taps_ref[...].astype(jnp.float32)
-    for k in range(KS * KS):
-        for l in range(LB):
-            tap_ref[l, k] = jnp.broadcast_to(t[k:k + 1, l * 128:(l + 1) * 128], (8, 128))
+    fill_taps(taps_ref, tap_ref)
     x_copy[0].wait()
     x_copy[1].start()
     for copy in w1_copy:
@@ -162,7 +220,7 @@
 
         def step(n, _):
             if g < groups:
-                conv_lane(n, r_bufs[g % 2], tap_ref, sp_ref, pr_ref, g)
+                conv_lane(n, r_bufs[g % 2], tap_ref, sp_ref, pr_ref, x_tmp, y_tmp, g)
             if g >= 1:
                 hidden_chunk(n, sn_ref, w1_ref, ph_ref, g - 1)
             return 0
@@ -191,6 +249,7 @@
 CODED = D + 128
 FAR_NEGATIVE = -1e30
 MESH = pl.DeviceIdType.MESH
+PLACED = (0, 1, 3, 2)
 
 
 def row_norm(values):
@@ -212,7 +271,7 @@
 
 
 def slide_layer(slides, ctxs, loads, emb_ref, slide_ref, pos_ref, len_ref, out_ref,
-                wqkv_ref, wout_ref, send_ref, recv_ref, rows_ref, k_ref, v_ref, q_ref, att_ref,
+                wqkv_ref, wout_ref, send_ref, recv_ref, rows_ref, k_ref, v_ref, q_ref, att_ref, peak_ref, sum_ref, acc_ref,
                 a2a_send, a2a_recv, own_sem, ring_send, ring_recv):
     load_qkv, load_out = loads
     count = slides * ctxs
@@ -265,7 +324,6 @@
 
     right = lax.rem(ctx + 1, ctxs)
     left = lax.rem(ctx + ctxs - 1, ctxs)
-    far = lax.rem(ctx + 2, ctxs)
     first, second = pl.ds(0, HALF_SEQ), pl.ds(HALF_SEQ, HALF_SEQ)
 
     def hop(n, blk, half, to):
@@ -273,9 +331,9 @@
             src_ref=rows_ref.at[blk, half], dst_ref=rows_ref.at[blk, half],
             send_sem=ring_send.at[n], recv_sem=ring_recv.at[n], device_id=(slide, to), device_id_type=MESH)
 
-    def keys_values(blk):
-        ln = row_norm(rows_ref[blk].astype(jnp.float32)).astype(jnp.bfloat16)
-        at = pl.ds(pl.multiple_of(blk * SEQ_DEV, 64), SEQ_DEV)
+    def keys_values(place):
+        ln = row_norm(rows_ref[lax.rem(ctx + PLACED[place], ctxs)].astype(jnp.float32)).astype(jnp.bfloat16)
+        at = slice(place * SEQ_DEV, (place + 1) * SEQ_DEV)
         k_ref[at, :] = jnp.dot(ln, wqkv_ref[:, D:2 * D], preferred_element_type=jnp.float32).astype(jnp.bfloat16)
         v_ref[at, :] = jnp.dot(ln, wqkv_ref[:, 2 * D:], preferred_element_type=jnp.float32).astype(jnp.bfloat16)
         return ln
@@ -283,44 +341,65 @@
     for h in own_hops:
         h.start()
     load_qkv.wait()
-    ln = keys_values(ctx)
+    ln = keys_values(0)
     q = jnp.dot(ln, wqkv_ref[:, :D], preferred_element_type=jnp.float32)
     q_ref[...] = (q.astype(jnp.bfloat16).astype(jnp.float32) * HEAD_DIM ** (-0.5)).astype(jnp.bfloat16)
+    length = len_ref[slide]
+    low = lax.broadcasted_iota(jnp.int32, (SEQ_DEV, 128), 1) < HEAD_DIM
+
+    def attend_part(place, blocks, first_part, last_part):
+        size = blocks * SEQ_DEV
+        lane = lax.broadcasted_iota(jnp.int32, (1, size), 1)
+        key = lane + lax.rem(ctx + PLACED[place], ctxs) * SEQ_DEV
+        if blocks == 2:
+            key = jnp.where(lane < SEQ_DEV, key, lane + (lax.rem(ctx + PLACED[place + 1], ctxs) - 1) * SEQ_DEV)
+        bias = jnp.where(key < length, 0.0, FAR_NEGATIVE)
+        at = slice(place * SEQ_DEV, place * SEQ_DEV + size)
+        for pair in range(HEADS // 2):
+            cols = slice(pair * 128, pair * 128 + 128)
+            q2 = q_ref[:, cols]
+            zero = jnp.zeros_like(q2)
+            both = jnp.concatenate([jnp.where(low, q2, zero), jnp.where(low, zero, q2)], axis=0)
+            s = lax.dot_general(both, k_ref[at, cols], (((1,), (1,)), ((), ())), preferred_element_type=jnp.float32) + bias
+            peak = jnp.max(s, axis=-1, keepdims=True)
+            if not first_part:
+                old = peak_ref[pair][:, :1]
+                peak = jnp.maximum(peak, old)
+                scale = jnp.exp(old - peak)
+            w = jnp.exp(s - peak)
+            denom = jnp.sum(w, axis=-1, keepdims=True)
+            o = jnp.dot(w.astype(jnp.bfloat16), v_ref[at, cols], preferred_element_type=jnp.float32)
+            if not first_part:
+                denom = denom + sum_ref[pair][:, :1] * scale
+                o = o + acc_ref[pair] * scale
+            if last_part:
+                o = o / denom
+                att_ref[:, cols] = jnp.where(low, o[:SEQ_DEV], o[SEQ_DEV:]).astype(jnp.bfloat16)
+            else:
+                peak_ref[pair] = jnp.broadcast_to(peak, (2 * SEQ_DEV, 128))
+                sum_ref[pair] = jnp.broadcast_to(denom, (2 * SEQ_DEV, 128))
+                acc_ref[pair] = o
+
     own_hops[0].wait_recv()
     onward = hop(4, left, first, right)
     onward.start()
     own_hops[1].wait_recv()
     back = hop(5, right, second, left)
     back.start()
+    attend_part(0, 1, True, False)
     own_hops[2].wait_recv()
     own_hops[3].wait_recv()
-
-    def near(n, _):
-        keys_values(lax.rem(ctx + 1 + 2 * n, ctxs))
-        return 0
-    lax.fori_loop(0, 2, near, 0)
+    keys_values(1)
+    keys_values(2)
+    attend_part(1, 2, False, False)
     onward.wait_recv()
     back.wait_recv()
-    keys_values(far)
+    keys_values(3)
+    attend_part(3, 1, False, True)
     for h in own_hops + [onward, back]:
         h.wait_send()
     whole.wait_send()
     load_out.wait()
-
-    length = len_ref[slide]
-    key = lax.broadcasted_iota(jnp.int32, (1, total), 1)
-    bias = jnp.where(key < length, 0.0, FAR_NEGATIVE)
-    low = lax.broadcasted_iota(jnp.int32, (SEQ_DEV, 128), 1) < HEAD_DIM
-    for pair in range(HEADS // 2):
-        cols = slice(pair * 128, pair * 128 + 128)
-        q2 = q_ref[:, cols]
-        zero = jnp.zeros_like(q2)
-        both = jnp.concatenate([jnp.where(low, q2, zero), jnp.where(low, zero, q2)], axis=0)
-        s = lax.dot_general(both, k_ref[:, cols], (((1,), (1,)), ((), ())), preferred_element_type=jnp.float32) + bias
-        w = jnp.exp(s - jnp.max(s, axis=-1, keepdims=True))
-        denom = jnp.sum(w, axis=-1, keepdims=True)
-        o = jnp.dot(w.astype(jnp.bfloat16), v_ref[:, cols], preferred_element_type=jnp.float32) / denom
-        att_ref[:, cols] = jnp.where(low, o[:SEQ_DEV], o[SEQ_DEV:]).astype(jnp.bfloat16)
     out = jnp.dot(att_ref[...], wout_ref[...], preferred_element_type=jnp.float32)
     out = out + rows_ref[ctx].astype(jnp.float32)
     row = lax.broadcasted_iota(jnp.int32, (SEQ_DEV, 1), 0) + ctx * SEQ_DEV
@@ -329,12 +408,12 @@
 
 def whole_kernel(groups, slides, ctxs, x_hbm, down_hbm, taps_ref, w1_hbm, w2_hbm, ls_ref, wqkv_hbm, wout_hbm,
                  slide_ref, pos_ref, len_ref, out_ref, emb_ref, load_sem, wqkv_ref, wout_ref, send_ref, recv_ref, rows_ref,
-                 k_ref, v_ref, q_ref, att_ref, a2a_send, a2a_recv, own_sem, ring_send, ring_recv, *encoder_refs):
+                 k_ref, v_ref, q_ref, att_ref, peak_ref, sum_ref, acc_ref, a2a_send, a2a_recv, own_sem, ring_send, ring_recv, *encoder_refs):
     greet(slides, ctxs)
     loads = (pltpu.make_async_copy(wqkv_hbm, wqkv_ref, load_sem.at[0]), pltpu.make_async_copy(wout_hbm, wout_ref, load_sem.at[1]))
     encode(groups, loads, x_hbm, down_hbm, taps_ref, w1_hbm, w2_hbm, ls_ref, emb_ref, *encoder_refs)
     slide_layer(slides, ctxs, loads, emb_ref, slide_ref, pos_ref, len_ref, out_ref,
-                wqkv_ref, wout_ref, send_ref, recv_ref, rows_ref, k_ref, v_ref, q_ref, att_ref,
+                wqkv_ref, wout_ref, send_ref, recv_ref, rows_ref, k_ref, v_ref, q_ref, att_ref, peak_ref, sum_ref, acc_ref,
                 a2a_send, a2a_recv, own_sem, ring_send, ring_recv)
 
 
@@ -358,6 +437,8 @@
             pltpu.VMEM((ctxs, SEQ_DEV, D), jnp.bfloat16),
             pltpu.VMEM((total, D), jnp.bfloat16), pltpu.VMEM((total, D), jnp.bfloat16),
             pltpu.VMEM((SEQ_DEV, D), jnp.bfloat16), pltpu.VMEM((SEQ_DEV, D), jnp.bfloat16),
+            pltpu.VMEM((HEADS // 2, 2 * SEQ_DEV, 128), jnp.float32), pltpu.VMEM((HEADS // 2, 2 * SEQ_DEV, 128), jnp.float32),
+            pltpu.VMEM((HEADS // 2, 2 * SEQ_DEV, 128), jnp.float32),
             pltpu.SemaphoreType.DMA, pltpu.SemaphoreType.DMA, pltpu.SemaphoreType.DMA,
             pltpu.SemaphoreType.DMA((6,)), pltpu.SemaphoreType.DMA((6,)),
             pltpu.VMEM((nt, 16, 16, C_IN), jnp.bfloat16),
@@ -371,12 +452,14 @@
             pltpu.VMEM((LB, 64, GROUP, 128), jnp.float32),
             pltpu.VMEM((LB, 64, GROUP, 128), jnp.float32),
             pltpu.VMEM((64 * GROUP, D), jnp.bfloat16),
-            pltpu.VMEM((LB, KS * KS, 8, 128), jnp.float32),
+            pltpu.VMEM((LB, len(TAP_SUMS), 8, 128), jnp.float32),
+            pltpu.VMEM((12, 3, 4, GROUP, 128), jnp.float32),
+            pltpu.VMEM((13, HALF, GROUP, 128), jnp.float32),
             pltpu.VMEM((LB, nt, HC), jnp.float32),
             pltpu.VMEM((LB, nt, 128), jnp.float32),
             pltpu.SemaphoreType.DMA((groups + 2 + LB,)),
         ],
-        compiler_params=pltpu.CompilerParams(collective_id=0, has_side_effects=True, vmem_limit_bytes=60 << 20),
+        compiler_params=pltpu.CompilerParams(collective_id=0, has_side_effects=True, vmem_limit_bytes=50 << 20),
         name="whole",
     )(x, down, taps, w1, w2, ls, qkv_weight[0], out_weight[0], tile_slide, tile_pos, slide_len)
 

time: 70.5 us -> 80.6 us (1.14)
  local copies, waits for them, and re-layouts: 1.69 us -> 7.19 us
  Pallas kernels: 68.6 us -> 73.1 us
    unnamed x1 -> x15, local copies, waits for them, and re-layouts: 1.69 us -> 7.19 us
    pallas_call x1, Pallas kernels: 68.6 us -> 73.1 us  [shards(): pl.pallas_call(functools.partial(whole_kernel, groups, slides, ctxs), out...]
where the time goes in v5:
time: 80.6 us; the launch traced here: 80.3 us
  Pallas kernels  73.1 us (91%)
  local copies, waits for them, and re-layouts  7.19 us (9%)
    pallas_call x1, Pallas kernels, shards(): pl.pallas_call(functools.partial(whole_kernel, groups, slides, ctxs), out...  73.1 us
    unnamed x15, local copies, waits for them, and re-layouts  7.19 us

profile of v5, /device:TPU:1, one launch (start us, length us, event | category | flops | bytes accessed | tf_op | source)
XLA Modules:
  0.0 80.3 jit_solution(13394673556495442928)
XLA Ops:
  0.0 0.0 copy-start
  0.0 1.7 %copy-done = bf16[1536,768]{1,0:T(8,128)(2,1)S(1)} copy-done((bf16[1536,768]{1,0:T(8,128)(2,1)S(1)}, bf16[1536,768]{1,0:T(8,128)(2,1)}, u32[]{:S(2)}) %copy-start) | copy-done | bytes 2359320
  1.7 0.0 copy-start.1
  1.7 1.3 %copy-done.1 = bf16[1,768,768]{2,1,0:T(8,128)(2,1)S(1)} copy-done((bf16[1,768,768]{2,1,0:T(8,128)(2,1)S(1)}, bf16[1,768,768]{2,1,0:T(8,128)(2,1)}, u32[]{:S(2)}) %copy-start.1) | copy-done | bytes 1179672
  2.9 0.0 copy-start.2
  2.9 0.9 %copy-done.2 = bf16[49,768]{1,0:T(8,128)(2,1)S(1)} copy-done((bf16[49,768]{1,0:T(8,128)(2,1)S(1)}, bf16[49,768]{1,0:T(8,128)(2,1)}, u32[]{:S(2)}) %copy-start.2) | copy-done | bytes 75288
  3.8 0.0 copy-start.3
  3.8 0.7 copy-done.3
  4.5 0.0 copy-start.4
  4.5 0.7 copy-done.4
  5.2 0.0 copy-start.5
  5.2 0.7 copy-done.5
  5.8 0.0 copy-start.6
  5.8 0.7 copy-done.6
  6.5 73.1 %whole.1 = bf16[192,768]{1,0:T(8,128)(2,1)S(1)} custom-call(bf16[32,16,16,384]{3,2,1,0:T(8,128)(2,1)} %x_hbm.1, bf16[1536,768]{1,0:T(8,128)(2,1)S(1)} %copy-done, bf16[49,768]{1,0:T(8,128)(2,1)S(1)} %copy-done.2, bf16[768,3072]{1,0:T(8,128)(2,1)} %w1_hbm.1, bf16[3072,768]{1,0:T(8,128)(2,1)} %w2_hbm.1, f32[768]{0:T(1024)S(1)} %copy-done.3, ...), custom_call_target="tpu_custom_call" | custom-call | tf_op jit(solution)/shard_map/whole/pallas_call | solution.py:428
  79.6 0.7 copy.13
Async XLA Ops:
  0.0 1.7 %copy-start = (bf16[1536,768]{1,0:T(8,128)(2,1)S(1)}, bf16[1536,768]{1,0:T(8,128)(2,1)}, u32[]{:S(2)}) copy-start(bf16[1536,768]{1,0:T(8,128)(2,1)} %down_hbm.1) | copy-start | bytes 7077892
  1.7 1.3 %copy-start.1 = (bf16[1,768,768]{2,1,0:T(8,128)(2,1)S(1)}, bf16[1,768,768]{2,1,0:T(8,128)(2,1)}, u32[]{:S(2)}) copy-start(bf16[1,768,768]{2,1,0:T(8,128)(2,1)} %param.18) | copy-start | bytes 3538948
  2.9 0.9 %copy-start.2 = (bf16[49,768]{1,0:T(8,128)(2,1)S(1)}, bf16[49,768]{1,0:T(8,128)(2,1)}, u32[]{:S(2)}) copy-start(bf16[49,768]{1,0:T(8,128)(2,1)} %taps_ref.1) | copy-start | bytes 225796
  3.8 0.7 copy-start.3
  4.5 0.7 copy-start.4
  5.2 0.7 copy-start.5
  5.8 0.7 copy-start.6

commit v6 on v5

--- a/solution.py
+++ b/solution.py
@@ -249,7 +249,6 @@
 CODED = D + 128
 FAR_NEGATIVE = -1e30
 MESH = pl.DeviceIdType.MESH
-PLACED = (0, 1, 3, 2)
 
 
 def row_norm(values):
@@ -271,7 +270,7 @@
 
 
 def slide_layer(slides, ctxs, loads, emb_ref, slide_ref, pos_ref, len_ref, out_ref,
-                wqkv_ref, wout_ref, send_ref, recv_ref, rows_ref, k_ref, v_ref, q_ref, att_ref, peak_ref, sum_ref, acc_ref,
+                wqkv_ref, wout_ref, send_ref, recv_ref, rows_ref, k_ref, v_ref, q_ref, att_ref,
                 a2a_send, a2a_recv, own_sem, ring_send, ring_recv):
     load_qkv, load_out = loads
     count = slides * ctxs
@@ -324,6 +323,7 @@
 
     right = lax.rem(ctx + 1, ctxs)
     left = lax.rem(ctx + ctxs - 1, ctxs)
+    far = lax.rem(ctx + 2, ctxs)
     first, second = pl.ds(0, HALF_SEQ), pl.ds(HALF_SEQ, HALF_SEQ)
 
     def hop(n, blk, half, to):
@@ -331,9 +331,9 @@
             src_ref=rows_ref.at[blk, half], dst_ref=rows_ref.at[blk, half],
             send_sem=ring_send.at[n], recv_sem=ring_recv.at[n], device_id=(slide, to), device_id_type=MESH)
 
-    def keys_values(place):
-        ln = row_norm(rows_ref[lax.rem(ctx + PLACED[place], ctxs)].astype(jnp.float32)).astype(jnp.bfloat16)
-        at = slice(place * SEQ_DEV, (place + 1) * SEQ_DEV)
+    def keys_values(blk):
+        ln = row_norm(rows_ref[blk].astype(jnp.float32)).astype(jnp.bfloat16)
+        at = pl.ds(pl.multiple_of(blk * SEQ_DEV, 64), SEQ_DEV)
         k_ref[at, :] = jnp.dot(ln, wqkv_ref[:, D:2 * D], preferred_element_type=jnp.float32).astype(jnp.bfloat16)
         v_ref[at, :] = jnp.dot(ln, wqkv_ref[:, 2 * D:], preferred_element_type=jnp.float32).astype(jnp.bfloat16)
         return ln
@@ -341,65 +341,44 @@
     for h in own_hops:
         h.start()
     load_qkv.wait()
-    ln = keys_values(0)
+    ln = keys_values(ctx)
     q = jnp.dot(ln, wqkv_ref[:, :D], preferred_element_type=jnp.float32)
     q_ref[...] = (q.astype(jnp.bfloat16).astype(jnp.float32) * HEAD_DIM ** (-0.5)).astype(jnp.bfloat16)
-    length = len_ref[slide]
-    low = lax.broadcasted_iota(jnp.int32, (SEQ_DEV, 128), 1) < HEAD_DIM
-
-    def attend_part(place, blocks, first_part, last_part):
-        size = blocks * SEQ_DEV
-        lane = lax.broadcasted_iota(jnp.int32, (1, size), 1)
-        key = lane + lax.rem(ctx + PLACED[place], ctxs) * SEQ_DEV
-        if blocks == 2:
-            key = jnp.where(lane < SEQ_DEV, key, lane + (lax.rem(ctx + PLACED[place + 1], ctxs) - 1) * SEQ_DEV)
-        bias = jnp.where(key < length, 0.0, FAR_NEGATIVE)
-        at = slice(place * SEQ_DEV, place * SEQ_DEV + size)
-        for pair in range(HEADS // 2):
-            cols = slice(pair * 128, pair * 128 + 128)
-            q2 = q_ref[:, cols]
-            zero = jnp.zeros_like(q2)
-            both = jnp.concatenate([jnp.where(low, q2, zero), jnp.where(low, zero, q2)], axis=0)
-            s = lax.dot_general(both, k_ref[at, cols], (((1,), (1,)), ((), ())), preferred_element_type=jnp.float32) + bias
-            peak = jnp.max(s, axis=-1, keepdims=True)
-            if not first_part:
-                old = peak_ref[pair][:, :1]
-                peak = jnp.maximum(peak, old)
-                scale = jnp.exp(old - peak)
-            w = jnp.exp(s - peak)
-            denom = jnp.sum(w, axis=-1, keepdims=True)
-            o = jnp.dot(w.astype(jnp.bfloat16), v_ref[at, cols], preferred_element_type=jnp.float32)
-            if not first_part:
-                denom = denom + sum_ref[pair][:, :1] * scale
-                o = o + acc_ref[pair] * scale
-            if last_part:
-                o = o / denom
-                att_ref[:, cols] = jnp.where(low, o[:SEQ_DEV], o[SEQ_DEV:]).astype(jnp.bfloat16)
-            else:
-                peak_ref[pair] = jnp.broadcast_to(peak, (2 * SEQ_DEV, 128))
-                sum_ref[pair] = jnp.broadcast_to(denom, (2 * SEQ_DEV, 128))
-                acc_ref[pair] = o
-
     own_hops[0].wait_recv()
     onward = hop(4, left, first, right)
     onward.start()
     own_hops[1].wait_recv()
     back = hop(5, right, second, left)
     back.start()
-    attend_part(0, 1, True, False)
     own_hops[2].wait_recv()
     own_hops[3].wait_recv()
-    keys_values(1)
-    keys_values(2)
-    attend_part(1, 2, False, False)
+
+    def near(n, _):
+        keys_values(lax.rem(ctx + 1 + 2 * n, ctxs))
+        return 0
+    lax.fori_loop(0, 2, near, 0)
     onward.wait_recv()
     back.wait_recv()
-    keys_values(3)
-    attend_part(3, 1, False, True)
+    keys_values(far)
     for h in own_hops + [onward, back]:
         h.wait_send()
     whole.wait_send()
     load_out.wait()
+
+    length = len_ref[slide]
+    key = lax.broadcasted_iota(jnp.int32, (1, total), 1)
+    bias = jnp.where(key < length, 0.0, FAR_NEGATIVE)
+    low = lax.broadcasted_iota(jnp.int32, (SEQ_DEV, 128), 1) < HEAD_DIM
+    for pair in range(HEADS // 2):
+        cols = slice(pair * 128, pair * 128 + 128)
+        q2 = q_ref[:, cols]
+        zero = jnp.zeros_like(q2)
+        both = jnp.concatenate([jnp.where(low, q2, zero), jnp.where(low, zero, q2)], axis=0)
+        s = lax.dot_general(both, k_ref[:, cols], (((1,), (1,)), ((), ())), preferred_element_type=jnp.float32) + bias
+        w = jnp.exp(s - jnp.max(s, axis=-1, keepdims=True))
+        denom = jnp.sum(w, axis=-1, keepdims=True)
+        o = jnp.dot(w.astype(jnp.bfloat16), v_ref[:, cols], preferred_element_type=jnp.float32) * (1.0 / denom)
+        att_ref[:, cols] = jnp.where(low, o[:SEQ_DEV], o[SEQ_DEV:]).astype(jnp.bfloat16)
     out = jnp.dot(att_ref[...], wout_ref[...], preferred_element_type=jnp.float32)
     out = out + rows_ref[ctx].astype(jnp.float32)
     row = lax.broadcasted_iota(jnp.int32, (SEQ_DEV, 1), 0) + ctx * SEQ_DEV
@@ -408,12 +387,12 @@
 
 def whole_kernel(groups, slides, ctxs, x_hbm, down_hbm, taps_ref, w1_hbm, w2_hbm, ls_ref, wqkv_hbm, wout_hbm,
                  slide_ref, pos_ref, len_ref, out_ref, emb_ref, load_sem, wqkv_ref, wout_ref, send_ref, recv_ref, rows_ref,
-                 k_ref, v_ref, q_ref, att_ref, peak_ref, sum_ref, acc_ref, a2a_send, a2a_recv, own_sem, ring_send, ring_recv, *encoder_refs):
+                 k_ref, v_ref, q_ref, att_ref, a2a_send, a2a_recv, own_sem, ring_send, ring_recv, *encoder_refs):
     greet(slides, ctxs)
     loads = (pltpu.make_async_copy(wqkv_hbm, wqkv_ref, load_sem.at[0]), pltpu.make_async_copy(wout_hbm, wout_ref, load_sem.at[1]))
     encode(groups, loads, x_hbm, down_hbm, taps_ref, w1_hbm, w2_hbm, ls_ref, emb_ref, *encoder_refs)
     slide_layer(slides, ctxs, loads, emb_ref, slide_ref, pos_ref, len_ref, out_ref,
-                wqkv_ref, wout_ref, send_ref, recv_ref, rows_ref, k_ref, v_ref, q_ref, att_ref, peak_ref, sum_ref, acc_ref,
+                wqkv_ref, wout_ref, send_ref, recv_ref, rows_ref, k_ref, v_ref, q_ref, att_ref,
                 a2a_send, a2a_recv, own_sem, ring_send, ring_recv)
 
 
@@ -437,8 +416,6 @@
             pltpu.VMEM((ctxs, SEQ_DEV, D), jnp.bfloat16),
             pltpu.VMEM((total, D), jnp.bfloat16), pltpu.VMEM((total, D), jnp.bfloat16),
             pltpu.VMEM((SEQ_DEV, D), jnp.bfloat16), pltpu.VMEM((SEQ_DEV, D), jnp.bfloat16),
-            pltpu.VMEM((HEADS // 2, 2 * SEQ_DEV, 128), jnp.float32), pltpu.VMEM((HEADS // 2, 2 * SEQ_DEV, 128), jnp.float32),
-            pltpu.VMEM((HEADS // 2, 2 * SEQ_DEV, 128), jnp.float32),
             pltpu.SemaphoreType.DMA, pltpu.SemaphoreType.DMA, pltpu.SemaphoreType.DMA,
             pltpu.SemaphoreType.DMA((6,)), pltpu.SemaphoreType.DMA((6,)),
             pltpu.VMEM((nt, 16, 16, C_IN), jnp.bfloat16),
@@ -459,7 +436,7 @@
             pltpu.VMEM((LB, nt, 128), jnp.float32),
             pltpu.SemaphoreType.DMA((groups + 2 + LB,)),
         ],
-        compiler_params=pltpu.CompilerParams(collective_id=0, has_side_effects=True, vmem_limit_bytes=50 << 20),
+        compiler_params=pltpu.CompilerParams(collective_id=0, has_side_effects=True, vmem_limit_bytes=60 << 20),
         name="whole",
     )(x, down, taps, w1, w2, ls, qkv_weight[0], out_weight[0], tile_slide, tile_pos, slide_len)
 

time: 80.6 us -> 69 us (0.86)
  Pallas kernels: 73.1 us -> 67.1 us
  local copies, waits for them, and re-layouts: 7.19 us -> 1.69 us
    pallas_call x1, Pallas kernels: 73.1 us -> 67.1 us  [shards(): pl.pallas_call(functools.partial(whole_kernel, groups, slides, ctxs), out...]
    unnamed x15 -> x1, local copies, waits for them, and re-layouts: 7.19 us -> 1.69 us
where the time goes in v6:
time: 69 us; the launch traced here: 68.8 us
  Pallas kernels  67.1 us (97%)
  local copies, waits for them, and re-layouts  1.69 us (2%)
    pallas_call x1, Pallas kernels, shards(): pl.pallas_call(functools.partial(whole_kernel, groups, slides, ctxs), out...  67.1 us
    unnamed x1, local copies, waits for them, and re-layouts  1.69 us

profile of v6, /device:TPU:1, one launch (start us, length us, event | category | flops | bytes accessed | tf_op | source)
XLA Modules:
  0.0 68.8 jit_solution(13543606237563483494)
XLA Ops:
  0.0 67.1 %whole.1 = bf16[192,768]{1,0:T(8,128)(2,1)} custom-call(bf16[32,16,16,384]{3,2,1,0:T(8,128)(2,1)} %x_hbm.1, bf16[1536,768]{1,0:T(8,128)(2,1)} %down_hbm.1, bf16[49,768]{1,0:T(8,128)(2,1)} %taps_ref.1, bf16[768,3072]{1,0:T(8,128)(2,1)} %w1_hbm.1, bf16[3072,768]{1,0:T(8,128)(2,1)} %w2_hbm.1, f32[768]{0:T(1024)} %ls_ref.1, bf16[768,2304]{1,0:T(8,128)(2,1)} %bitcast.2, ...), custom_call_target="tpu_custom_call" | custom-call | tf_op jit(solution)/shard_map/whole/pallas_call | solution.py:407
  67.1 1.7 %copy.13 = bf16[192,768]{1,0:T(8,128)(2,1)} copy(bf16[192,768]{1,0:T(8,128)(2,1)} %whole.1) | data formatting | bytes 589824

commit v7 on v6

--- a/solution.py
+++ b/solution.py
@@ -376,8 +376,9 @@
         both = jnp.concatenate([jnp.where(low, q2, zero), jnp.where(low, zero, q2)], axis=0)
         s = lax.dot_general(both, k_ref[:, cols], (((1,), (1,)), ((), ())), preferred_element_type=jnp.float32) + bias
         w = jnp.exp(s - jnp.max(s, axis=-1, keepdims=True))
-        denom = jnp.sum(w, axis=-1, keepdims=True)
-        o = jnp.dot(w.astype(jnp.bfloat16), v_ref[:, cols], preferred_element_type=jnp.float32) * (1.0 / denom)
+        ext = jnp.concatenate([v_ref[:, cols], jnp.full((total, 128), 1.0, jnp.bfloat16)], axis=1)
+        o = jnp.dot(w.astype(jnp.bfloat16), ext, preferred_element_type=jnp.float32)
+        o = o[:, :128] * (1.0 / o[:, 128:])
         att_ref[:, cols] = jnp.where(low, o[:SEQ_DEV], o[SEQ_DEV:]).astype(jnp.bfloat16)
     out = jnp.dot(att_ref[...], wout_ref[...], preferred_element_type=jnp.float32)
     out = out + rows_ref[ctx].astype(jnp.float32)

time: 69 us -> 68.8 us (level)
  no operation moved by 1% of the time
where the time goes in v7:
time: 68.8 us; the launch traced here: 68.7 us
  Pallas kernels  67 us (97%)
  local copies, waits for them, and re-layouts  1.69 us (2%)
    pallas_call x1, Pallas kernels, shards(): pl.pallas_call(functools.partial(whole_kernel, groups, slides, ctxs), out...  67 us
    unnamed x1, local copies, waits for them, and re-layouts  1.69 us

profile of v7, /device:TPU:1, one launch (start us, length us, event | category | flops | bytes accessed | tf_op | source)
XLA Modules:
  0.0 68.7 jit_solution(16631458249174062831)
XLA Ops:
  0.0 67.0 %whole.1 = bf16[192,768]{1,0:T(8,128)(2,1)} custom-call(bf16[32,16,16,384]{3,2,1,0:T(8,128)(2,1)} %x_hbm.1, bf16[1536,768]{1,0:T(8,128)(2,1)} %down_hbm.1, bf16[49,768]{1,0:T(8,128)(2,1)} %taps_ref.1, bf16[768,3072]{1,0:T(8,128)(2,1)} %w1_hbm.1, bf16[3072,768]{1,0:T(8,128)(2,1)} %w2_hbm.1, f32[768]{0:T(1024)} %ls_ref.1, bf16[768,2304]{1,0:T(8,128)(2,1)} %bitcast.2, ...), custom_call_target="tpu_custom_call" | custom-call | tf_op jit(solution)/shard_map/whole/pallas_call | solution.py:408
  67.0 1.7 %copy.13 = bf16[192,768]{1,0:T(8,128)(2,1)} copy(bf16[192,768]{1,0:T(8,128)(2,1)} %whole.1) | data formatting | bytes 589824
